TPU v7x, 32 devices: a whole 2x2x4 slice. The times are simulated.
32 devices in a mesh: lat: 8 (over z, y), lon: 2 (over x), comp: 2 (over core).
Axes of the slice: x: 2, y: 2, z: 4, core: 2. Of those that a mesh axis runs over, the one named last changes fastest.
Arguments:
- atm_state: bfloat16 [192, 256, 384], P('lat', ('lon', 'comp')), may hold values from -6 to 6
- ocean_state: bfloat16 [192, 256, 256], P(('lat', 'comp'), 'lon'), may hold values from -6 to 6
- wet_mask: int32 [192, 256], P(('lat', 'comp'), 'lon'), may hold values 0 or 1
- legendre: bfloat16 [512, 384, 192], P(('lat', 'lon', 'comp')), may hold values from -4 to 4
- quad_weight: float32 [192], replicated, may hold values from 0.5 to 2
- spec_real: bfloat16 [384, 384], replicated, may hold values from -0.3125 to 0.3125
- spec_imag: bfloat16 [384, 384], replicated, may hold values from -0.3125 to 0.3125
- degree_gain: float32 [384], replicated, may hold values from 0.5 to 2
- atm_gain: float32 [2, 384], replicated, may hold values from 0.1 to 1.9
- atm_up: bfloat16 [384, 768], replicated, may hold values from -0.3125 to 0.3125
- atm_down: bfloat16 [768, 384], replicated, may hold values from -0.21875 to 0.21875
- atm_to_surface: bfloat16 [384, 32], replicated, may hold values from -0.3125 to 0.3125
- surface_to_atm: bfloat16 [32, 384], replicated, may hold values from -1 to 1
- ocean_to_surface: bfloat16 [256, 32], replicated, may hold values from -0.375 to 0.375
- surface_to_ocean: bfloat16 [32, 256], replicated, may hold values from -1 to 1
- ocean_kernel: bfloat16 [2, 7, 7, 256], replicated, may hold values from -0.875 to 0.875
- ocean_gain: float32 [2, 256], replicated, may hold values from 0.1 to 1.9
- ocean_up: bfloat16 [2, 256, 1024], replicated, may hold values from -0.375 to 0.375
- ocean_down: bfloat16 [2, 1024, 256], replicated, may hold values from -0.1875 to 0.1875
Outputs:
- atm_out: bfloat16 [192, 256, 384], P('lat', ('lon', 'comp'))
- ocean_out: bfloat16 [192, 256, 256], P(('lat', 'comp'), 'lon')
All inputs are finite; a program needn't handle non-finite values. No bound on the sum of `wet_mask` on one device may be relied on, other than what follows from the above.
Results may differ from a plain program's by a relative error of at most 0.01.
Values may be sent and summed in bfloat16 or wider, within the bound.
A program may use at most 128 MiB of HBM per device.

v0:
```python
import functools
import math

import jax
import jax.numpy as jnp
import numpy as np
from jax import lax
from jax.experimental import pallas as pl
from jax.experimental.pallas import tpu as pltpu
from jax.sharding import PartitionSpec as P

MODES = 512
STENCIL_TAPS = 7
OCEAN_DILATION = 2
COLUMNS = ("lon", "comp")
EVERY = ("lat", "lon", "comp")


epsilon = 1e-05


def padded(block, sides, width):
    for axis, dim in sides:
        count = lax.axis_size(axis)
        forward = [(i, i + 1) for i in range(count - 1)]
        backward = [(target, source) for source, target in forward]
        low = lax.ppermute(
            lax.slice_in_dim(block, block.shape[dim] - width, None, axis=dim), axis, forward
        )
        high = lax.ppermute(lax.slice_in_dim(block, 0, width, axis=dim), axis, backward)
        block = jnp.concatenate([low, block, high], axis=dim)
    return block


def layer_norm(values, gain):
    centred = values - jnp.mean(values, axis=-1, keepdims=True)
    spread = jnp.mean(centred * centred, axis=-1, keepdims=True)
    return centred * lax.rsqrt(spread + epsilon) * gain


def wave_table(row_index, circle):
    longitude = jnp.arange(circle, dtype=jnp.int32)
    wavenumber = row_index // 2
    phases = wavenumber[:, None] * longitude[None, :] % circle
    angles = phases.astype(jnp.float32) * (2.0 * math.pi / circle)
    waves = jnp.where((row_index % 2 == 0)[:, None], jnp.cos(angles), -jnp.sin(angles))
    return (wavenumber, waves)


def forward_table(row_index, circle):
    _, waves = wave_table(row_index, circle)
    return (waves.T / math.sqrt(circle)).astype(jnp.bfloat16)


def inverse_table(row_index, circle):
    wavenumber, waves = wave_table(row_index, circle)
    factor = jnp.where(wavenumber == 0, 1.0, 2.0).astype(jnp.float32)
    return (waves * factor[:, None] / math.sqrt(circle)).astype(jnp.bfloat16)


def reorder_rows(total_rows, owned, lat_count, col_count):
    positions = jnp.arange(total_rows, dtype=jnp.int32)
    stride = lat_count * owned
    return (
        owned * (positions % stride // owned * col_count + positions // stride) + positions % owned
    )


def spectral_filter(gathered, table, quad_weight, spec_real, spec_imag, degree_gain):
    count = table.shape[0]
    lat_total = table.shape[2]
    channels = gathered.shape[2]
    split_parts = gathered.reshape(lat_total, count, 2, channels)
    weighted = (table.astype(jnp.float32) * (quad_weight / lat_total)).astype(jnp.bfloat16)
    coeffs = jnp.einsum(
        "mln,nmpc->mplc", weighted, split_parts, preferred_element_type=jnp.float32
    ).astype(jnp.bfloat16)
    real_part = coeffs[:, 0]
    imag_part = coeffs[:, 1]
    mixed_real = jnp.dot(real_part, spec_real, preferred_element_type=jnp.float32) - jnp.dot(
        imag_part, spec_imag, preferred_element_type=jnp.float32
    )
    mixed_imag = jnp.dot(real_part, spec_imag, preferred_element_type=jnp.float32) + jnp.dot(
        imag_part, spec_real, preferred_element_type=jnp.float32
    )
    scaled = (jnp.stack([mixed_real, mixed_imag], axis=1) * degree_gain[:, None]).astype(
        jnp.bfloat16
    )
    returned = jnp.einsum(
        "mln,mplc->nmpc", table, scaled, preferred_element_type=jnp.float32
    ).astype(jnp.bfloat16)
    return returned.reshape(lat_total, 2 * count, channels)


def folds(circle, lat_dev, col_count, devices):
    return (
        MODES == 2 * circle
        and lat_dev % col_count == 0
        and devices % 4 == 0
        and (circle // 2) % devices == 0
        and (MODES // devices) % 4 == 0
    )


def place_of(kind, i, group):
    return kind * group + (group - 1 - i if kind % 2 else i)


def folded_waves(circle, devices):
    longitude = jnp.arange(circle, dtype=jnp.int32)
    position = jnp.arange(circle, dtype=jnp.int32)
    group = devices // 4
    owned = circle // devices
    owner = position // owned
    kind, place = owner // group, owner % group
    place = jnp.where(kind % 2 == 1, group - 1 - place, place)
    row_index = (4 * place + kind) * owned + position % owned
    wavenumber = jnp.where(row_index == 1, circle // 2, row_index // 2)
    phases = wavenumber[:, None] * longitude[None, :] % circle
    angles = phases.astype(jnp.float32) * (2.0 * math.pi / circle)
    cosine = ((row_index % 2 == 0) | (row_index == 1))[:, None]
    return jnp.where(cosine, jnp.cos(angles), -jnp.sin(angles)) / math.sqrt(circle)


def folded_operators(table, quad_weight, degree_gain):
    devices = lax.axis_size(EVERY)
    me = lax.axis_index(EVERY)
    count, _, lat_total = table.shape
    group = devices // 4
    part = count // 4
    family = me // group
    scaled = (table.astype(jnp.float32) * degree_gain[:, None]).astype(jnp.bfloat16)
    operators = jnp.einsum(
        "mlt,mlu->mtu", table, scaled, preferred_element_type=jnp.float32
    )
    operators = operators * (quad_weight / lat_total)
    first_scale = jnp.where(me == 0, 0.5, 1.0).astype(jnp.float32)
    scales = jnp.where(jnp.arange(count) == 0, first_scale, 1.0)
    operators = (operators * scales[:, None, None]).astype(jnp.bfloat16)
    turn = []
    for base in (group, 3 * group):
        for i in range(group):
            turn.append((base + (i + 1) % group, base + i))
    rotated = lax.ppermute(operators[:1], EVERY, turn)
    mirrored = jnp.concatenate([rotated, jnp.flip(operators[1:], axis=0)], axis=0)
    ordered = jnp.where(family % 2 == 1, mirrored, operators)
    received = [lax.dynamic_slice_in_dim(ordered, family * part, part, axis=0)]
    for shift in range(1, 4):
        pairs = []
        for i in range(group):
            for kind in range(4):
                pairs.append((place_of(kind, i, group), place_of(kind ^ shift, i, group)))
        piece = lax.dynamic_slice_in_dim(ordered, (family ^ shift) * part, part, axis=0)
        received.append(lax.ppermute(piece, EVERY, pairs))
    received = [value.astype(jnp.float32) for value in received]
    same = received[0] + received[2]
    other = received[1] + received[3]
    direct = jnp.where(family % 2 == 0, same, other)
    mirror = jnp.where(family % 2 == 0, other, same)
    lone = ((me == 0) & (jnp.arange(part) == 0))[:, None, None]
    both = direct + mirror
    gap = jnp.where(lone, 0.0, direct - mirror)
    top = jnp.concatenate([jnp.where(lone, direct, both), -gap], axis=2)
    bottom = jnp.concatenate([gap, jnp.where(lone, mirror, both)], axis=2)
    return (2.0 * top).astype(jnp.bfloat16), (2.0 * bottom).astype(jnp.bfloat16)


def folded_spectral(normed, legendre, quad_weight, spec_real, spec_imag, degree_gain, circle):
    width = normed.shape[2]
    top, bottom = folded_operators(legendre, quad_weight, degree_gain)
    slots = top.shape[0]
    waves = folded_waves(circle, lax.axis_size(EVERY)).astype(jnp.bfloat16)
    columns = lax.all_to_all(normed, COLUMNS, split_axis=0, concat_axis=1, tiled=True)
    spectrum = jnp.einsum(
        "rn,tnc->trc", waves, columns, preferred_element_type=jnp.float32
    ).astype(jnp.bfloat16)
    gathered = lax.all_to_all(spectrum, EVERY, split_axis=1, concat_axis=0, tiled=True)
    lat_total = gathered.shape[0]
    channels = jnp.concatenate([spec_real, spec_imag], axis=1)
    turned = gathered.reshape(lat_total, slots, 2, width).transpose(1, 2, 0, 3)
    mixed = jnp.dot(turned, channels, preferred_element_type=jnp.float32).astype(jnp.bfloat16)
    upper = jnp.concatenate([mixed[:, 0, :, :width], mixed[:, 1, :, width:]], axis=1)
    lower = jnp.concatenate([mixed[:, 0, :, width:], mixed[:, 1, :, :width]], axis=1)
    cosine = jnp.einsum("stu,suc->stc", top, upper, preferred_element_type=jnp.float32)
    sine = jnp.einsum("stu,suc->stc", bottom, lower, preferred_element_type=jnp.float32)
    filtered = jnp.stack([cosine, sine], axis=1).astype(jnp.bfloat16)
    filtered = filtered.reshape(2 * slots, lat_total, width).transpose(1, 0, 2)
    returned = lax.all_to_all(filtered, EVERY, split_axis=0, concat_axis=1, tiled=True)
    spatial = jnp.einsum(
        "rn,trc->tnc", waves, returned, preferred_element_type=jnp.float32
    ).astype(jnp.bfloat16)
    spectral = lax.all_to_all(spatial, COLUMNS, split_axis=1, concat_axis=0, tiled=True)
    return spectral, (spectrum, filtered)


def plain_spectral(normed, legendre, quad_weight, spec_real, spec_imag, degree_gain, circle):
    lat_count = lax.axis_size("lat")
    col_count = lax.axis_size(("lon", "comp"))
    total_rows = 2 * MODES
    owned = 2 * legendre.shape[0]
    natural = jnp.arange(total_rows, dtype=jnp.int32)
    columns = lax.all_to_all(normed, ("lon", "comp"), split_axis=2, concat_axis=1, tiled=True)
    forward = forward_table(natural, circle)
    inverse = inverse_table(reorder_rows(total_rows, owned, lat_count, col_count), circle)
    spectrum = jnp.einsum(
        "anc,nr->arc", columns, forward, preferred_element_type=jnp.float32
    ).astype(jnp.bfloat16)
    gathered = lax.all_to_all(
        lax.all_to_all(spectrum, "lat", split_axis=1, concat_axis=0, tiled=True),
        ("lon", "comp"),
        split_axis=1,
        concat_axis=2,
        tiled=True,
    )
    filtered = spectral_filter(gathered, legendre, quad_weight, spec_real, spec_imag, degree_gain)
    returned = lax.all_to_all(
        lax.all_to_all(filtered, "lat", split_axis=0, concat_axis=1, tiled=True),
        ("lon", "comp"),
        split_axis=2,
        concat_axis=1,
        tiled=True,
    )
    spatial = jnp.einsum(
        "arc,rn->anc", returned, inverse, preferred_element_type=jnp.float32
    ).astype(jnp.bfloat16)
    spectral = lax.all_to_all(spatial, COLUMNS, split_axis=1, concat_axis=2, tiled=True)
    return spectral, (spectrum, filtered)


def ocean_block(padded_field, kernel, gain, up_weight, down_weight):
    stencil_reach = STENCIL_TAPS // 2 * OCEAN_DILATION
    tile_height = padded_field.shape[0] - 2 * stencil_reach
    tile_breadth = padded_field.shape[1] - 2 * stencil_reach
    stencil = jnp.zeros((tile_height, tile_breadth, padded_field.shape[2]), jnp.float32)
    for row_offset_tap in range(STENCIL_TAPS):
        for column_tap in range(STENCIL_TAPS):
            stencil_window = padded_field[
                row_offset_tap * OCEAN_DILATION : row_offset_tap * OCEAN_DILATION + tile_height,
                column_tap * OCEAN_DILATION : column_tap * OCEAN_DILATION + tile_breadth,
            ]
            stencil = stencil + stencil_window.astype(jnp.float32) * kernel[
                row_offset_tap, column_tap
            ].astype(jnp.float32)
    normed = layer_norm(stencil, gain).astype(jnp.bfloat16)
    hidden = jax.nn.gelu(jnp.dot(normed, up_weight, preferred_element_type=jnp.float32)).astype(
        jnp.bfloat16
    )
    centre = padded_field[
        stencil_reach : stencil_reach + tile_height, stencil_reach : stencil_reach + tile_breadth
    ]
    return (
        centre.astype(jnp.float32)
        + jnp.dot(hidden, down_weight, preferred_element_type=jnp.float32)
    ).astype(jnp.bfloat16)


def ocean_kernel_body(
    field_ref, taps_ref, gain_ref, up_ref, down_ref, after_ref, out_ref, wide, normed
):
    rows, cols, width = out_ref.shape
    step = OCEAN_DILATION
    lanes = 128

    @pl.loop(0, rows + (STENCIL_TAPS - 1) * step)
    def _(row):
        wide[row] = field_ref[row].astype(jnp.float32)

    @pl.loop(0, rows // 2)
    def _(pair):
        base = pair // step * (2 * step) + pair % step
        for half in range(width // lanes):
            part = slice(half * lanes, (half + 1) * lanes)
            sums = [jnp.zeros((cols, lanes), jnp.float32) for _ in range(2)]
            for a in range(STENCIL_TAPS + 1):
                for b in range(STENCIL_TAPS):
                    window = wide[base + a * step, b * step : b * step + cols, part]
                    for which in range(2):
                        tap = a - which
                        if 0 <= tap < STENCIL_TAPS:
                            weight = taps_ref[tap * STENCIL_TAPS + b, :, part]
                            sums[which] = sums[which] + window * weight
            for which in range(2):
                normed[which * cols : (which + 1) * cols, part] = sums[which]
        stencil = normed[...]
        values = layer_norm(stencil, gain_ref[...]).astype(jnp.bfloat16)
        hidden = jax.nn.gelu(
            jnp.dot(values, up_ref[...], preferred_element_type=jnp.float32)
        ).astype(jnp.bfloat16)
        moved = jnp.dot(hidden, down_ref[...], preferred_element_type=jnp.float32)
        reach = STENCIL_TAPS // 2 * step
        for which in range(2):
            row = base + which * step
            centre = wide[row + reach, reach : reach + cols, :]
            out_ref[row] = (centre + moved[which * cols : (which + 1) * cols]).astype(
                out_ref.dtype
            )


def fast_ocean_block(field, kernel, gain, up_weight, down_weight, after):
    reach = STENCIL_TAPS // 2 * OCEAN_DILATION
    rows, cols, width = field.shape[0] - 2 * reach, field.shape[1] - 2 * reach, field.shape[2]
    hidden = up_weight.shape[1]
    taps = kernel.astype(jnp.float32).reshape(STENCIL_TAPS * STENCIL_TAPS, 1, width)
    whole = pl.BlockSpec(memory_space=pltpu.VMEM)
    cells = rows * cols
    return pl.pallas_call(
        ocean_kernel_body,
        out_shape=jax.ShapeDtypeStruct((rows, cols, width), jnp.bfloat16),
        in_specs=[whole] * 5 + [pl.BlockSpec(memory_space=pl.ANY)],
        out_specs=whole,
        scratch_shapes=[
            pltpu.VMEM(field.shape, jnp.float32),
            pltpu.VMEM((2 * cols, width), jnp.float32),
        ],
        compiler_params=pltpu.CompilerParams(vmem_limit_bytes=32 * 1024 * 1024),
        cost_estimate=pl.CostEstimate(
            flops=4 * cells * width * hidden + 98 * cells * width * 64,
            bytes_accessed=4 * field.size + 4 * up_weight.size,
            transcendentals=cells * hidden,
        ),
    )(field, taps, gain[None, :], up_weight, down_weight, after)


MESH_ID = pl.DeviceIdType.MESH


def fits(atm_state, ocean_state, legendre):
    devices = lax.axis_size(EVERY)
    col_count = lax.axis_size(COLUMNS)
    lat_dev, lon_dev, width = atm_state.shape
    rows, cols, sea_width = ocean_state.shape
    circle = lon_dev * col_count
    reach = STENCIL_TAPS // 2 * OCEAN_DILATION
    return (
        folds(circle, lat_dev, col_count, devices)
        and lax.axis_size("lon") == 2
        and lax.axis_size("comp") == 2
        and circle // devices == 8
        and legendre.shape[0] == 16
        and lat_dev // col_count % 2 == 0
        and lat_dev == 2 * rows
        and cols == 2 * lon_dev
        and cols == 128
        and rows == 2 * reach
        and rows % (2 * OCEAN_DILATION) == 0
        and 128 < legendre.shape[2] <= 192
        and lon_dev % 16 == 0
        and width % 128 == 0
        and sea_width == 256
    )


def whole_step_body(
    lat_total,
    atm_hbm,
    sea_hbm,
    wet_ref,
    legendre_hbm,
    quad_ref,
    real_hbm,
    imag_hbm,
    degree_ref,
    gain_ref,
    up_hbm,
    down_hbm,
    to_sea_ref,
    from_sea_ref,
    to_air_ref,
    from_air_ref,
    taps_in_ref,
    sea_gain_ref,
    sea_up_hbm,
    sea_down_hbm,
    waves_hbm,
    waves_back_hbm,
    air_out,
    sea_out,
    air,
    sea,
    legendre,
    spec_real,
    spec_imag,
    air_up,
    air_down,
    sea_up,
    sea_down,
    waves,
    waves_back,
    taps,
    wet_square,
    wet_full,
    flux_out,
    flux_in,
    forced,
    normed,
    columns,
    spec_send,
    gathered,
    flat,
    returned,
    spatial,
    spectral,
    op_send,
    op_recv,
    op_lone,
    op_lone_recv,
    both,
    gap,
    field,
    edges,
    sides,
    wide,
    stencil,
    load_sem,
    local_sem,
    flux_sem,
    column_sem,
    owner_sem,
    back_sem,
    grid_sem,
    op_sem,
    halo_sem,
):
    f32, bf16 = jnp.float32, jnp.bfloat16
    lat = lax.axis_index("lat")
    lon = lax.axis_index("lon")
    comp = lax.axis_index("comp")
    col_count = lax.axis_size(COLUMNS)
    devices = lax.axis_size(EVERY)
    group = devices // 4
    col = lon * 2 + comp
    me = lat * col_count + col
    tile = lat * 2 + comp
    tiles = lax.axis_size("lat") * 2
    lat_dev, lon_dev, width = air.shape
    rows, cols, sea_width = sea.shape
    band = lat_dev // col_count
    pairs = band // 2
    circle = lon_dev * col_count
    step = OCEAN_DILATION
    reach = STENCIL_TAPS // 2 * step
    slots = both.shape[0]
    block = 256

    def at_device(index):
        return (index // col_count, index % col_count // 2, index % 2)

    def at_tile(index, side):
        return (index // 2, side, index % 2)

    def remote(source, target, sems, k, where):
        return pltpu.make_async_remote_copy(
            src_ref=source,
            dst_ref=target,
            send_sem=sems.at[0, k],
            recv_sem=sems.at[1, k],
            device_id=where,
            device_id_type=MESH_ID,
        )

    barrier = pltpu.get_barrier_semaphore()

    @pl.loop(1, devices)
    def _(k):
        pl.semaphore_signal(
            barrier, inc=1, device_id=at_device((me + k) % devices), device_id_type=MESH_ID
        )

    loads = {}
    for index, (name, source, target) in enumerate(
        (
            ("sea", sea_hbm, sea),
            ("air", atm_hbm, air),
            ("legendre", legendre_hbm, legendre),
            ("waves", waves_hbm, waves),
            ("sea_up", sea_up_hbm, sea_up),
            ("sea_down", sea_down_hbm, sea_down),
            ("real", real_hbm, spec_real),
            ("imag", imag_hbm, spec_imag),
            ("back", waves_back_hbm, waves_back),
            ("up", up_hbm, air_up),
            ("down", down_hbm, air_down),
        )
    ):
        loads[name] = pltpu.make_async_copy(source, target, load_sem.at[index])
        loads[name].start()

    wet_square[...] = jnp.zeros_like(wet_square)
    wet_square[0:rows, :] = wet_ref[...].astype(f32)
    turned = jnp.transpose(wet_square[...])
    for i in range(rows):
        wet_full[i] = jnp.broadcast_to(turned[:, i : i + 1], (cols, 128))

    loads["sea"].wait()

    @pl.loop(0, rows)
    def _(i):
        flux = jnp.dot(sea[i], to_air_ref[...], preferred_element_type=f32)
        flux = (flux * wet_full[i][:, 0 : flux.shape[1]]).astype(bf16)
        flux_out[0, 0, i] = flux[0:lon_dev]
        flux_out[0, 1, i] = flux[lon_dev : 2 * lon_dev]

    loads["air"].wait()

    @pl.loop(0, rows // 2)
    def _(i):
        for half in range(2):
            block_of = air[pl.ds(half * rows + 2 * i, 2)].reshape(2 * lon_dev, width)
            flux = jnp.dot(block_of, to_sea_ref[...], preferred_element_type=f32).astype(bf16)
            flux_out[1, half, 2 * i] = flux[0:lon_dev]
            flux_out[1, half, 2 * i + 1] = flux[lon_dev : 2 * lon_dev]

    pl.semaphore_wait(barrier, devices - 1)
    partner = (lat, lon, 1 - comp)
    moves = []
    for kind in range(2):
        moves.append(
            remote(
                flux_out.at[kind, 1 - comp], flux_in.at[kind, comp], flux_sem, kind, partner
            )
        )
        moves[-1].start()
    kept = []
    for kind in range(2):
        kept.append(
            pltpu.make_async_copy(
                flux_out.at[kind, comp], flux_in.at[kind, comp], local_sem.at[kind]
            )
        )
        kept[-1].start()

    for k in range(2):
        for a in range(STENCIL_TAPS):
            line = taps_in_ref[k, a].astype(f32)
            for b in range(STENCIL_TAPS):
                taps[(k * STENCIL_TAPS + a) * STENCIL_TAPS + b] = line[b : b + 1]

    for move in kept:
        move.wait()
    for move in moves:
        move.wait()

    per = block // lon_dev

    @pl.loop(0, lat_dev // per)
    def _(i):
        half = i // (rows // per)
        start = i % (rows // per) * per
        flux = flux_in[0, half, pl.ds(start, per)].reshape(block, -1)
        value = air[pl.ds(i * per, per)].reshape(block, width).astype(f32)
        value = value + jnp.dot(flux, from_sea_ref[...], preferred_element_type=f32)
        forced[pl.ds(i * per, per)] = value.reshape(per, lon_dev, width)
        value = layer_norm(value, gain_ref[0:1]).astype(bf16)
        normed[pl.ds(i * per, per)] = value.reshape(per, lon_dev, width)

    to_columns = []
    for k in range(1, col_count):
        other = (col + k) % col_count
        move = remote(
            normed.at[pl.ds(other * band, band)],
            columns.at[col],
            column_sem,
            k - 1,
            (lat, other // 2, other % 2),
        )
        move.start()
        to_columns.append(move)
    own_columns = pltpu.make_async_copy(
        normed.at[pl.ds(col * band, band)], columns.at[col], local_sem.at[0]
    )
    own_columns.start()

    @pl.loop(0, rows)
    def _(i):
        flux = jnp.concatenate([flux_in[1, 0, i], flux_in[1, 1, i]], axis=0)
        added = jnp.dot(flux, from_air_ref[...], preferred_element_type=f32)
        mask = wet_full[i]
        mask = jnp.concatenate([mask, mask], axis=1)
        field[0, i] = (sea[i].astype(f32) + mask * added).astype(bf16)

    strip = 16
    near = pl.multiple_of((cols - strip) * (1 - lon), strip)

    def halo_moves(k):
        source = field.at[k]
        strips = source.at[:, pl.ds(near, strip), :]
        low, high = pl.ds(0, reach), pl.ds(rows - reach, reach)
        side = remote(
            strips, sides.at[k, pl.ds(reach, rows)], halo_sem.at[k], 0, at_tile(tile, 1 - lon)
        )
        back = (
            remote(source.at[low], edges.at[k, 1], halo_sem.at[k], 1, at_tile(tile - 1, lon)),
            remote(
                source.at[low, pl.ds(near, strip), :],
                sides.at[k, pl.ds(reach + rows, reach)],
                halo_sem.at[k],
                2,
                at_tile(tile - 1, 1 - lon),
            ),
        )
        ahead = (
            remote(source.at[high], edges.at[k, 0], halo_sem.at[k], 3, at_tile(tile + 1, lon)),
            remote(
                source.at[high, pl.ds(near, strip), :],
                sides.at[k, pl.ds(0, reach)],
                halo_sem.at[k],
                4,
                at_tile(tile + 1, 1 - lon),
            ),
        )
        return side, back, ahead

    def send_halo(k):
        side, back, ahead = halo_moves(k)

        @pl.when(tile > 0)
        def _():
            for move in back:
                move.start()

        @pl.when(tile < tiles - 1)
        def _():
            for move in ahead:
                move.start()

        side.start()

    def take_halo(k):
        side, back, ahead = halo_moves(k)
        side.wait()

        @pl.when(tile > 0)
        def _():
            for move in back:
                move.wait_send()
            for move in ahead:
                move.wait_recv()

        @pl.when(tile < tiles - 1)
        def _():
            for move in ahead:
                move.wait_send()
            for move in back:
                move.wait_recv()

        def margins(row, values):
            left = jnp.where(lon == 1, values[8:16], 0.0)
            right = jnp.where(lon == 0, values[0:8], 0.0)
            wide[row, 0:8] = left
            wide[row, cols + 8 : cols + 16] = right

        @pl.loop(0, rows)
        def _(i):
            wide[reach + i, 8 : cols + 8] = field[k, i].astype(f32)
            margins(reach + i, sides[k, reach + i].astype(f32))

        for which in range(2):
            first = which * (reach + rows)
            present = tile > 0 if which == 0 else tile < tiles - 1

            @pl.when(present)
            def _():
                @pl.loop(0, reach)
                def _(i):
                    wide[first + i, 8 : cols + 8] = edges[k, which, i].astype(f32)
                    margins(first + i, sides[k, first + i].astype(f32))

            @pl.when(jnp.logical_not(present))
            def _():
                @pl.loop(0, reach)
                def _(i):
                    wide[first + i] = jnp.zeros(wide.shape[1:], f32)

    send_halo(0)

    loads["legendre"].wait()
    kind = me // group
    odd = kind % 2
    place = me % group
    count = legendre.shape[0]
    edge = lat_total - 128

    def operator(k):
        index = odd * ((count - k) % count) + (1 - odd) * k
        table = legendre[index]
        scaled = (table.astype(f32) * degree_ref[...]).astype(bf16)
        value = lax.dot_general(
            table, scaled, (((0,), (0,)), ((), ())), preferred_element_type=f32
        )
        value = value * jnp.where((me == 0) & (index == 0), 0.5, 1.0).astype(f32)
        return (value * (quad_ref[...] / lat_total)).astype(bf16)

    @pl.loop(0, count // 2)
    def _(k):
        which, spot = k // 2, k % 2
        first, second = operator(2 * k), operator(2 * k + 1)
        op_send[which, 2 * spot] = first[:, 0:128]
        op_send[which, 2 * spot + 1] = second[:, 0:128]
        tail = jnp.concatenate([first[:, 128:lat_total], second[:, 128:lat_total]], axis=1)
        op_send[which, 4 + spot, :, 0 : 2 * edge] = tail

        @pl.when(k == 0)
        def _():
            op_lone[0] = first[:, 0:128]
            op_lone[1, :, 0 : 2 * edge] = tail

    spot_of = odd * (group - 1 - place) + (1 - odd) * place
    op_moves = []
    for shift, other in ((1, kind + 1 - 2 * odd), (2, (kind + 2) % 4), (3, 3 - kind)):
        other_odd = other % 2
        there = other * group + other_odd * (group - 1 - spot_of) + (1 - other_odd) * spot_of
        move = remote(
            op_send.at[other], op_recv.at[shift - 1], op_sem, shift - 1, at_device(there)
        )
        move.start()
        op_moves.append(move)
    lone_move = remote(
        op_lone, op_lone_recv.at[kind // 2], op_sem, 3 + kind // 2, at_device((group - place) % group)
    )

    @pl.when(odd == 1)
    def _():
        lone_move.start()

    def sea_pairs(k, first, last):
        @pl.loop(first, last)
        def _(pair):
            base = pair // step * (2 * step) + pair % step
            for half in range(sea_width // 128):
                part = slice(half * 128, (half + 1) * 128)
                sums = [jnp.zeros((cols, 128), f32) for _ in range(2)]
                for a in range(STENCIL_TAPS + 1):
                    for b in range(STENCIL_TAPS):
                        start = 8 - reach + b * step
                        window = wide[base + a * step, start : start + cols, part]
                        for which in range(2):
                            tap = a - which
                            if 0 <= tap < STENCIL_TAPS:
                                weight = taps[
                                    (k * STENCIL_TAPS + tap) * STENCIL_TAPS + b, :, part
                                ]
                                sums[which] = sums[which] + window * weight
                for which in range(2):
                    stencil[which * cols : (which + 1) * cols, part] = sums[which]
            values = layer_norm(stencil[...], sea_gain_ref[k : k + 1]).astype(bf16)
            hidden = jax.nn.gelu(
                jnp.dot(values, sea_up[k], preferred_element_type=f32)
            ).astype(bf16)
            moved = jnp.dot(hidden, sea_down[k], preferred_element_type=f32)
            for which in range(2):
                row = base + which * step
                centre = wide[row + reach, 8 : 8 + cols, :]
                value = (centre + moved[which * cols : (which + 1) * cols]).astype(bf16)
                if k == 0:
                    field[1, row] = value
                else:
                    mask = wet_full[row]
                    mask = jnp.concatenate([mask, mask], axis=1)
                    sea_out[row] = jnp.where(mask > 0.5, value, sea[row])

    take_halo(0)
    loads["sea_up"].wait()
    loads["sea_down"].wait()
    sea_pairs(0, 0, 2)

    loads["waves"].wait()
    own_columns.wait()
    for move in to_columns:
        move.wait()

    def transform(t):
        lines = jnp.concatenate([columns[b, t] for b in range(col_count)], axis=0)
        value = jnp.dot(waves[...], lines, preferred_element_type=f32)
        return value.reshape(devices, 8, width)

    @pl.loop(0, pairs)
    def _(p):
        joined = jnp.concatenate([transform(2 * p), transform(2 * p + 1)], axis=1)
        spec_send[:, p] = joined.astype(bf16)

    def exchange(source, target, sems):
        def move(k):
            other = (me + k) % devices
            return remote(source.at[other], target.at[me], sems, k, at_device(other))

        return move

    to_owner = exchange(spec_send, gathered, owner_sem)

    @pl.loop(1, devices)
    def _(k):
        to_owner(k).start()

    own = pltpu.make_async_copy(spec_send.at[me], gathered.at[me], local_sem.at[1])
    own.start()

    sea_pairs(0, 2, rows // 2)
    send_halo(1)

    for move in op_moves:
        move.wait()

    @pl.when(odd == 1)
    def _():
        lone_move.wait_send()

    @pl.when(kind == 0)
    def _():
        for which in range(2):
            remote(
                op_lone, op_lone_recv.at[which], op_sem, 3 + which, at_device(me)
            ).wait_recv()
            op_recv[2 * which, 0] = op_lone_recv[which, 0]
            op_recv[2 * which, 4, :, 0:edge] = op_lone_recv[which, 1, :, 0:edge]

    for s in range(slots):
        lone = (me == 0) & (s == 0)
        for piece in range(2):
            if piece == 0:
                into = slice(0, 128)

                def part_of(ref):
                    return ref[s].astype(f32)

            else:
                into = slice(128, lat_total)

                def part_of(ref):
                    lanes = slice(s % 2 * edge, (s % 2 + 1) * edge)
                    return ref[4 + s // 2, :, lanes].astype(f32)

            same = part_of(op_send.at[kind]) + part_of(op_recv.at[1])
            other = part_of(op_recv.at[0]) + part_of(op_recv.at[2])
            direct = jnp.where(odd == 0, same, other)
            mirror = jnp.where(odd == 0, other, same)
            total = jnp.where(lone, direct, direct + mirror)
            rest = jnp.where(lone, mirror, direct + mirror)
            skew = jnp.where(lone, 0.0, direct - mirror)
            both[s, 0, :, into] = (2.0 * total).astype(bf16)
            both[s, 1, :, into] = (2.0 * rest).astype(bf16)
            gap[s, :, into] = (2.0 * skew).astype(bf16)

    loads["real"].wait()
    loads["imag"].wait()
    own.wait()

    @pl.loop(1, devices)
    def _(k):
        to_owner(k).wait()

    chunk = devices // 8
    lines = chunk * band * 8

    @pl.loop(0, 8)
    def _(i):
        value = gathered[pl.ds(i * chunk, chunk)].astype(f32).reshape(lines, width)
        for c in range(width // 128):
            flat[c, pl.ds(i * lines, lines), :] = value[:, c * 128 : (c + 1) * 128]

    def take_rows(q):
        taken = [
            flat[c, pl.ds(q, lat_total, stride=8), :] for c in range(width // 128)
        ]
        return jnp.concatenate(taken, axis=1).astype(bf16)

    def put_rows(q, value):
        for c in range(width // 128):
            flat[c, pl.ds(q, lat_total, stride=8), :] = value[:, c * 128 : (c + 1) * 128]

    for s in range(slots):
        re, im = take_rows(2 * s), take_rows(2 * s + 1)

        def mix(value, matrix):
            return jnp.dot(value, matrix[...], preferred_element_type=f32).astype(bf16)

        def act(matrix, value):
            return jnp.dot(matrix, value, preferred_element_type=f32)

        cosine = act(both[s, 0], mix(re, spec_real)) - act(gap[s], mix(im, spec_imag))
        sine = act(gap[s], mix(re, spec_imag)) + act(both[s, 1], mix(im, spec_real))
        put_rows(2 * s, cosine)
        put_rows(2 * s + 1, sine)

    @pl.loop(0, 8)
    def _(i):
        value = [flat[c, pl.ds(i * lines, lines), :] for c in range(width // 128)]
        value = jnp.concatenate(value, axis=1).astype(bf16)
        gathered[pl.ds(i * chunk, chunk)] = value.reshape(chunk, pairs, 16, width)

    from_owner = exchange(gathered, returned, back_sem)

    @pl.loop(1, devices)
    def _(k):
        from_owner(k).start()

    own = pltpu.make_async_copy(gathered.at[me], returned.at[me], local_sem.at[0])
    own.start()

    take_halo(1)
    sea_pairs(1, 0, rows // 2)

    loads["back"].wait()
    own.wait()

    @pl.loop(1, devices)
    def _(k):
        from_owner(k).wait()

    @pl.loop(0, pairs)
    def _(p):
        value = returned[:, p].astype(f32)
        for which in range(2):
            lines = value[:, 8 * which : 8 * which + 8].reshape(circle, width).astype(bf16)
            line = jnp.dot(waves_back[...], lines, preferred_element_type=f32).astype(bf16)
            for b in range(col_count):
                spatial[b, 2 * p + which] = line[b * lon_dev : (b + 1) * lon_dev]

    to_grid = []
    for k in range(1, col_count):
        other = (col + k) % col_count
        move = remote(
            spatial.at[other],
            spectral.at[pl.ds(col * band, band)],
            grid_sem,
            k - 1,
            (lat, other // 2, other % 2),
        )
        move.start()
        to_grid.append(move)
    own = pltpu.make_async_copy(
        spatial.at[col], spectral.at[pl.ds(col * band, band)], local_sem.at[1]
    )
    own.start()

    loads["up"].wait()
    loads["down"].wait()
    own.wait()
    for move in to_grid:
        move.wait()

    @pl.loop(0, lat_dev // per)
    def _(i):
        here = pl.ds(i * per, per)
        mixed = forced[here].reshape(block, width)
        mixed = mixed + spectral[here].reshape(block, width).astype(f32)
        value = layer_norm(mixed, gain_ref[1:2]).astype(bf16)
        hidden = jax.nn.gelu(
            jnp.dot(value, air_up[...], preferred_element_type=f32)
        ).astype(bf16)
        mixed = mixed + jnp.dot(hidden, air_down[...], preferred_element_type=f32)
        air_out[here] = mixed.astype(bf16).reshape(per, lon_dev, width)


def whole_step(
    atm_state,
    ocean_state,
    wet_mask,
    legendre,
    quad_weight,
    spec_real,
    spec_imag,
    degree_gain,
    atm_gain,
    atm_up,
    atm_down,
    atm_to_surface,
    surface_to_atm,
    ocean_to_surface,
    surface_to_ocean,
    ocean_kernel,
    ocean_gain,
    ocean_up,
    ocean_down,
):
    bf16, f32 = jnp.bfloat16, jnp.float32
    devices = lax.axis_size(EVERY)
    col_count = lax.axis_size(COLUMNS)
    lat_dev, lon_dev, width = atm_state.shape
    rows, cols, sea_width = ocean_state.shape
    circle = lon_dev * col_count
    lat_total = legendre.shape[2]
    band = lat_dev // col_count
    reach = STENCIL_TAPS // 2 * OCEAN_DILATION
    slots = legendre.shape[0] // 4
    surface = atm_to_surface.shape[1]
    with jax.ensure_compile_time_eval():
        table = np.asarray(folded_waves(circle, devices).astype(f32))
    waves = jnp.asarray(table, f32).astype(bf16)
    waves_back = jnp.asarray(table.T, f32).astype(bf16)
    vmem = pl.BlockSpec(memory_space=pltpu.VMEM)
    hbm = pl.BlockSpec(memory_space=pl.ANY)
    tall = (devices, band // 2, 16, width)
    squares = (lat_total, 128)
    dma = pltpu.SemaphoreType.DMA
    return pl.pallas_call(
        functools.partial(whole_step_body, lat_total),
        out_shape=(
            jax.ShapeDtypeStruct(atm_state.shape, bf16),
            jax.ShapeDtypeStruct(ocean_state.shape, bf16),
        ),
        in_specs=[
            hbm, hbm, vmem, hbm, vmem, hbm, hbm, vmem, vmem, hbm, hbm,
            vmem, vmem, vmem, vmem, vmem, vmem, hbm, hbm, hbm, hbm,
        ],
        out_specs=(vmem, vmem),
        scratch_shapes=[
            pltpu.VMEM(atm_state.shape, bf16),
            pltpu.VMEM(ocean_state.shape, bf16),
            pltpu.VMEM(legendre.shape, bf16),
            pltpu.VMEM(spec_real.shape, bf16),
            pltpu.VMEM(spec_imag.shape, bf16),
            pltpu.VMEM(atm_up.shape, bf16),
            pltpu.VMEM(atm_down.shape, bf16),
            pltpu.VMEM(ocean_up.shape, bf16),
            pltpu.VMEM(ocean_down.shape, bf16),
            pltpu.VMEM(waves.shape, bf16),
            pltpu.VMEM(waves.shape, bf16),
            pltpu.VMEM((2 * STENCIL_TAPS * STENCIL_TAPS, 1, sea_width), f32),
            pltpu.VMEM((128, 128), f32),
            pltpu.VMEM((rows, cols, 128), f32),
            pltpu.VMEM((2, 2, rows, lon_dev, surface), bf16),
            pltpu.VMEM((2, 2, rows, lon_dev, surface), bf16),
            pltpu.VMEM(atm_state.shape, f32),
            pltpu.VMEM(atm_state.shape, bf16),
            pltpu.VMEM((col_count, band, lon_dev, width), bf16),
            pltpu.VMEM(tall, bf16),
            pltpu.VMEM(tall, bf16),
            pltpu.VMEM((width // 128, devices * band * 8, 128), f32),
            pltpu.VMEM(tall, bf16),
            pltpu.VMEM((col_count, band, lon_dev, width), bf16),
            pltpu.VMEM(atm_state.shape, bf16),
            pltpu.VMEM((4, 6) + squares, bf16),
            pltpu.VMEM((3, 6) + squares, bf16),
            pltpu.VMEM((2,) + squares, bf16),
            pltpu.VMEM((2, 2) + squares, bf16),
            pltpu.VMEM((slots, 2, lat_total, lat_total), bf16),
            pltpu.VMEM((slots, lat_total, lat_total), bf16),
            pltpu.VMEM((2,) + ocean_state.shape, bf16),
            pltpu.VMEM((2, 2, reach, cols, sea_width), bf16),
            pltpu.VMEM((2, rows + 2 * reach, 16, sea_width), bf16),
            pltpu.VMEM((rows + 2 * reach, cols + 16, sea_width), f32),
            pltpu.VMEM((2 * cols, sea_width), f32),
            dma((11,)),
            dma((2,)),
            dma((2, 2)),
            dma((2, 3)),
            dma((2, devices)),
            dma((2, devices)),
            dma((2, 3)),
            dma((2, 5)),
            dma((2, 2, 5)),
        ],
        compiler_params=pltpu.CompilerParams(
            collective_id=0, has_side_effects=True, vmem_limit_bytes=60 * 1024 * 1024
        ),
    )(
        atm_state,
        ocean_state,
        wet_mask,
        legendre,
        quad_weight[None, :],
        spec_real,
        spec_imag,
        degree_gain[:, None],
        atm_gain,
        atm_up,
        atm_down,
        atm_to_surface,
        surface_to_atm,
        ocean_to_surface,
        surface_to_ocean,
        ocean_kernel,
        ocean_gain,
        ocean_up,
        ocean_down,
        waves,
        waves_back,
    )


def local(
    atm_state,
    ocean_state,
    wet_mask,
    legendre,
    quad_weight,
    spec_real,
    spec_imag,
    degree_gain,
    atm_gain,
    atm_up,
    atm_down,
    atm_to_surface,
    surface_to_atm,
    ocean_to_surface,
    surface_to_ocean,
    ocean_kernel,
    ocean_gain,
    ocean_up,
    ocean_down,
):
    col_count = lax.axis_size(COLUMNS)
    lat_dev, lon_dev, _ = atm_state.shape
    circle = lon_dev * col_count
    if fits(atm_state, ocean_state, legendre):
        return whole_step(
            atm_state,
            ocean_state,
            wet_mask,
            legendre,
            quad_weight,
            spec_real,
            spec_imag,
            degree_gain,
            atm_gain,
            atm_up,
            atm_down,
            atm_to_surface,
            surface_to_atm,
            ocean_to_surface,
            surface_to_ocean,
            ocean_kernel,
            ocean_gain,
            ocean_up,
            ocean_down,
        )
    wet = wet_mask.astype(jnp.float32)[:, :, None]
    ocean_flux = (
        jnp.dot(ocean_state, ocean_to_surface, preferred_element_type=jnp.float32) * wet
    ).astype(jnp.bfloat16)
    atm_flux = jnp.dot(atm_state, atm_to_surface, preferred_element_type=jnp.float32).astype(
        jnp.bfloat16
    )
    flux_here = lax.all_to_all(ocean_flux, "comp", split_axis=1, concat_axis=0, tiled=True)
    flux_sea = lax.all_to_all(atm_flux, "comp", split_axis=0, concat_axis=1, tiled=True)
    forced = atm_state.astype(jnp.float32) + jnp.dot(
        flux_here, surface_to_atm, preferred_element_type=jnp.float32
    )
    normed = layer_norm(forced, atm_gain[0]).astype(jnp.bfloat16)
    run_spectral = (
        folded_spectral
        if folds(circle, lat_dev, col_count, lax.axis_size(EVERY))
        else plain_spectral
    )
    spectral, stages = run_spectral(
        normed, legendre, quad_weight, spec_real, spec_imag, degree_gain, circle
    )
    mixed = forced + spectral.astype(jnp.float32)
    normed_two = layer_norm(mixed, atm_gain[1]).astype(jnp.bfloat16)
    hidden = jax.nn.gelu(jnp.dot(normed_two, atm_up, preferred_element_type=jnp.float32)).astype(
        jnp.bfloat16
    )
    atm_out = (mixed + jnp.dot(hidden, atm_down, preferred_element_type=jnp.float32)).astype(
        jnp.bfloat16
    )
    ocean_in = (
        ocean_state.astype(jnp.float32)
        + wet * jnp.dot(flux_sea, surface_to_ocean, preferred_element_type=jnp.float32)
    ).astype(jnp.bfloat16)
    stencil_reach = STENCIL_TAPS // 2 * OCEAN_DILATION
    sides = ((("lat", "comp"), 0), ("lon", 1))
    current = ocean_in
    quick = ocean_in.shape[0] % (2 * OCEAN_DILATION) == 0 and ocean_in.shape[2] % 128 == 0
    for k in range(2):
        field = padded(current, sides, stencil_reach)
        weights = (ocean_kernel[k], ocean_gain[k], ocean_up[k], ocean_down[k])
        if quick:
            current = fast_ocean_block(field, *weights, stages[k])
        else:
            current = ocean_block(field, *weights)
    ocean_out = jnp.where(wet_mask[:, :, None] == 1, current, ocean_state)
    return (atm_out, ocean_out)


def solution(mesh):
    placed = (
        P("lat", ("lon", "comp"), None),
        P(("lat", "comp"), "lon", None),
        P(("lat", "comp"), "lon"),
        P(("lat", "lon", "comp"), None, None),
        P(),
        P(),
        P(),
        P(),
        P(),
        P(),
        P(),
        P(),
        P(),
        P(),
        P(),
        P(),
        P(),
        P(),
        P(),
    )

    return jax.shard_map(
        local,
        mesh=mesh,
        in_specs=placed,
        out_specs=(P("lat", ("lon", "comp"), None), P(("lat", "comp"), "lon", None)),
        check_vma=False,
    )
```

profile of v0, /device:TPU:13, one launch (start us, length us, event | category | flops | bytes accessed | tf_op | source)
XLA Modules:
  0.0 144.6 jit_solution(15570186899275524220)
XLA Ops:
  0.6 1.4 copy.31.taps_in_ref
  2.1 1.4 copy.30.to_air_ref
  3.5 1.5 %copy.29.to_sea_ref = bf16[384,32]{1,0:T(8,128)(2,1)} copy(bf16[384,32]{0,1:T(8,128)(2,1)} %param.32) | data formatting | bytes 49152 | tf_op args[11]
  5.0 1.5 %broadcast_in_dim.8.degree_ref = f32[384,1]{1,0:T(8,128)} reshape(f32[384]{0:T(512)} %param.28) | data formatting | bytes 3072 | tf_op jit(solution)/shard_map/broadcast_in_dim | solution.py:1064
  6.5 4.5 %copy.27.legendre_hbm = bf16[16,384,192]{2,1,0:T(8,128)(2,1)} copy(bf16[16,384,192]{1,2,0:T(8,128)(2,1)} %param.24) | data formatting | bytes 4718592 | tf_op args[3]
  10.9 130.3 %shard_map.212 = (bf16[24,64,384]{2,1,0:T(8,128)(2,1)}, bf16[12,128,256]{2,1,0:T(8,128)(2,1)}) custom-call(bf16[24,64,384]{2,1,0:T(8,128)(2,1)} %atm_hbm.1, bf16[12,128,256]{2,1,0:T(8,128)(2,1)} %sea_hbm.1, s32[12,128]{1,0:T(8,128)} %wet_ref.1, bf16[16,384,192]{2,1,0:T(8,128)(2,1)} %copy.27.legendre_hbm, f32[1,192]{1,0:T(1,128)} %bitcast.1, ...), custom_call_target="tpu_custom_call" | custom-call | tf_op jit(solution)/shard_map/pallas_call | solution.py:995
  141.2 0.0 copy-start
  141.2 2.5 %copy.34 = bf16[24,64,384]{2,1,0:T(8,128)(2,1)} copy(bf16[24,64,384]{2,1,0:T(8,128)(2,1)} %get-tuple-element.4) | data formatting | bytes 2359296
  143.7 0.0 copy-done
  143.7 0.9 copy.35
Async XLA Ops:
  141.2 2.5 %copy-start = (bf16[12,128,256]{2,1,0:T(8,128)(2,1)S(1)}, bf16[12,128,256]{2,1,0:T(8,128)(2,1)}, u32[]{:S(2)}) copy-start(bf16[12,128,256]{2,1,0:T(8,128)(2,1)} %get-tuple-element.5) | copy-start | bytes 2359300
where the time goes:
time: 145 us
  Pallas kernels  130 us (90%)
  local copies, waits for them, and re-layouts  13.7 us (9%)
    pallas_call x1, Pallas kernels, whole_step(): pl.pallas_call(functools.partial(whole_step_body, lat_total), out_shape=(...  130 us
    unnamed x8, local copies, waits for them, and re-layouts  12.2 us

commit v1 on v0

--- a/solution.py
+++ b/solution.py
@@ -342,8 +342,10 @@
         and cols == 2 * lon_dev
         and cols == 128
         and rows == 2 * reach
+        and reach % 2 == 0
         and rows % (2 * OCEAN_DILATION) == 0
         and 128 < legendre.shape[2] <= 192
+        and legendre.shape[2] % 16 == 0
         and lon_dev % 16 == 0
         and width % 128 == 0
         and sea_width == 256
@@ -397,17 +399,23 @@
     spec_send,
     gathered,
     flat,
+    turned_rows,
+    mixed_real,
+    mixed_imag,
+    filtered,
     returned,
     spatial,
     spectral,
     op_send,
     op_recv,
+    op_own,
     op_lone,
     op_lone_recv,
     both,
     gap,
     field,
     edges,
+    strips,
     sides,
     wide,
     stencil,
@@ -415,9 +423,13 @@
     local_sem,
     flux_sem,
     column_sem,
+    column_own,
     owner_sem,
+    owner_own,
     back_sem,
+    back_own,
     grid_sem,
+    grid_own,
     op_sem,
     halo_sem,
 ):
@@ -440,7 +452,6 @@
     step = OCEAN_DILATION
     reach = STENCIL_TAPS // 2 * step
     slots = both.shape[0]
-    block = 256
 
     def at_device(index):
         return (index // col_count, index % col_count // 2, index % 2)
@@ -449,14 +460,18 @@
         return (index // 2, side, index % 2)
 
     def remote(source, target, sems, k, where):
+        place_in = k if isinstance(k, tuple) else (k,)
         return pltpu.make_async_remote_copy(
             src_ref=source,
             dst_ref=target,
-            send_sem=sems.at[0, k],
-            recv_sem=sems.at[1, k],
+            send_sem=sems.at[(0,) + place_in],
+            recv_sem=sems.at[(1,) + place_in],
             device_id=where,
             device_id_type=MESH_ID,
         )
+
+    def across(left, right):
+        return lax.dot_general(left, right, (((1,), (1,)), ((), ())), preferred_element_type=f32)
 
     barrier = pltpu.get_barrier_semaphore()
 
@@ -469,9 +484,9 @@
     loads = {}
     for index, (name, source, target) in enumerate(
         (
+            ("legendre", legendre_hbm, legendre),
             ("sea", sea_hbm, sea),
             ("air", atm_hbm, air),
-            ("legendre", legendre_hbm, legendre),
             ("waves", waves_hbm, waves),
             ("sea_up", sea_up_hbm, sea_up),
             ("sea_down", sea_down_hbm, sea_down),
@@ -483,6 +498,7 @@
         )
     ):
         loads[name] = pltpu.make_async_copy(source, target, load_sem.at[index])
+    for name in ("legendre", "sea", "air"):
         loads[name].start()
 
     wet_square[...] = jnp.zeros_like(wet_square)
@@ -491,187 +507,11 @@
     for i in range(rows):
         wet_full[i] = jnp.broadcast_to(turned[:, i : i + 1], (cols, 128))
 
-    loads["sea"].wait()
-
-    @pl.loop(0, rows)
-    def _(i):
-        flux = jnp.dot(sea[i], to_air_ref[...], preferred_element_type=f32)
-        flux = (flux * wet_full[i][:, 0 : flux.shape[1]]).astype(bf16)
-        flux_out[0, 0, i] = flux[0:lon_dev]
-        flux_out[0, 1, i] = flux[lon_dev : 2 * lon_dev]
-
-    loads["air"].wait()
-
-    @pl.loop(0, rows // 2)
-    def _(i):
-        for half in range(2):
-            block_of = air[pl.ds(half * rows + 2 * i, 2)].reshape(2 * lon_dev, width)
-            flux = jnp.dot(block_of, to_sea_ref[...], preferred_element_type=f32).astype(bf16)
-            flux_out[1, half, 2 * i] = flux[0:lon_dev]
-            flux_out[1, half, 2 * i + 1] = flux[lon_dev : 2 * lon_dev]
-
-    pl.semaphore_wait(barrier, devices - 1)
-    partner = (lat, lon, 1 - comp)
-    moves = []
-    for kind in range(2):
-        moves.append(
-            remote(
-                flux_out.at[kind, 1 - comp], flux_in.at[kind, comp], flux_sem, kind, partner
-            )
-        )
-        moves[-1].start()
-    kept = []
-    for kind in range(2):
-        kept.append(
-            pltpu.make_async_copy(
-                flux_out.at[kind, comp], flux_in.at[kind, comp], local_sem.at[kind]
-            )
-        )
-        kept[-1].start()
-
-    for k in range(2):
-        for a in range(STENCIL_TAPS):
-            line = taps_in_ref[k, a].astype(f32)
-            for b in range(STENCIL_TAPS):
-                taps[(k * STENCIL_TAPS + a) * STENCIL_TAPS + b] = line[b : b + 1]
-
-    for move in kept:
-        move.wait()
-    for move in moves:
-        move.wait()
-
-    per = block // lon_dev
-
-    @pl.loop(0, lat_dev // per)
-    def _(i):
-        half = i // (rows // per)
-        start = i % (rows // per) * per
-        flux = flux_in[0, half, pl.ds(start, per)].reshape(block, -1)
-        value = air[pl.ds(i * per, per)].reshape(block, width).astype(f32)
-        value = value + jnp.dot(flux, from_sea_ref[...], preferred_element_type=f32)
-        forced[pl.ds(i * per, per)] = value.reshape(per, lon_dev, width)
-        value = layer_norm(value, gain_ref[0:1]).astype(bf16)
-        normed[pl.ds(i * per, per)] = value.reshape(per, lon_dev, width)
-
-    to_columns = []
-    for k in range(1, col_count):
-        other = (col + k) % col_count
-        move = remote(
-            normed.at[pl.ds(other * band, band)],
-            columns.at[col],
-            column_sem,
-            k - 1,
-            (lat, other // 2, other % 2),
-        )
-        move.start()
-        to_columns.append(move)
-    own_columns = pltpu.make_async_copy(
-        normed.at[pl.ds(col * band, band)], columns.at[col], local_sem.at[0]
-    )
-    own_columns.start()
-
-    @pl.loop(0, rows)
-    def _(i):
-        flux = jnp.concatenate([flux_in[1, 0, i], flux_in[1, 1, i]], axis=0)
-        added = jnp.dot(flux, from_air_ref[...], preferred_element_type=f32)
-        mask = wet_full[i]
-        mask = jnp.concatenate([mask, mask], axis=1)
-        field[0, i] = (sea[i].astype(f32) + mask * added).astype(bf16)
-
-    strip = 16
-    near = pl.multiple_of((cols - strip) * (1 - lon), strip)
-
-    def halo_moves(k):
-        source = field.at[k]
-        strips = source.at[:, pl.ds(near, strip), :]
-        low, high = pl.ds(0, reach), pl.ds(rows - reach, reach)
-        side = remote(
-            strips, sides.at[k, pl.ds(reach, rows)], halo_sem.at[k], 0, at_tile(tile, 1 - lon)
-        )
-        back = (
-            remote(source.at[low], edges.at[k, 1], halo_sem.at[k], 1, at_tile(tile - 1, lon)),
-            remote(
-                source.at[low, pl.ds(near, strip), :],
-                sides.at[k, pl.ds(reach + rows, reach)],
-                halo_sem.at[k],
-                2,
-                at_tile(tile - 1, 1 - lon),
-            ),
-        )
-        ahead = (
-            remote(source.at[high], edges.at[k, 0], halo_sem.at[k], 3, at_tile(tile + 1, lon)),
-            remote(
-                source.at[high, pl.ds(near, strip), :],
-                sides.at[k, pl.ds(0, reach)],
-                halo_sem.at[k],
-                4,
-                at_tile(tile + 1, 1 - lon),
-            ),
-        )
-        return side, back, ahead
-
-    def send_halo(k):
-        side, back, ahead = halo_moves(k)
-
-        @pl.when(tile > 0)
-        def _():
-            for move in back:
-                move.start()
-
-        @pl.when(tile < tiles - 1)
-        def _():
-            for move in ahead:
-                move.start()
-
-        side.start()
-
-    def take_halo(k):
-        side, back, ahead = halo_moves(k)
-        side.wait()
-
-        @pl.when(tile > 0)
-        def _():
-            for move in back:
-                move.wait_send()
-            for move in ahead:
-                move.wait_recv()
-
-        @pl.when(tile < tiles - 1)
-        def _():
-            for move in ahead:
-                move.wait_send()
-            for move in back:
-                move.wait_recv()
-
-        def margins(row, values):
-            left = jnp.where(lon == 1, values[8:16], 0.0)
-            right = jnp.where(lon == 0, values[0:8], 0.0)
-            wide[row, 0:8] = left
-            wide[row, cols + 8 : cols + 16] = right
-
-        @pl.loop(0, rows)
-        def _(i):
-            wide[reach + i, 8 : cols + 8] = field[k, i].astype(f32)
-            margins(reach + i, sides[k, reach + i].astype(f32))
-
-        for which in range(2):
-            first = which * (reach + rows)
-            present = tile > 0 if which == 0 else tile < tiles - 1
-
-            @pl.when(present)
-            def _():
-                @pl.loop(0, reach)
-                def _(i):
-                    wide[first + i, 8 : cols + 8] = edges[k, which, i].astype(f32)
-                    margins(first + i, sides[k, first + i].astype(f32))
-
-            @pl.when(jnp.logical_not(present))
-            def _():
-                @pl.loop(0, reach)
-                def _(i):
-                    wide[first + i] = jnp.zeros(wide.shape[1:], f32)
-
-    send_halo(0)
+    for a in range(STENCIL_TAPS):
+        for b in range(STENCIL_TAPS):
+            line = taps_in_ref[a, b].astype(f32)
+            for k in range(2):
+                taps[(k * STENCIL_TAPS + a) * STENCIL_TAPS + b] = line[k : k + 1]
 
     loads["legendre"].wait()
     kind = me // group
@@ -679,34 +519,53 @@
     place = me % group
     count = legendre.shape[0]
     edge = lat_total - 128
+    row_at = lax.broadcasted_iota(jnp.int32, (lat_total, lat_total), 0)
+    lane_at = lax.broadcasted_iota(jnp.int32, (lat_total, lat_total), 1)
+    upper, diagonal = row_at <= lane_at, row_at == lane_at
 
     def operator(k):
         index = odd * ((count - k) % count) + (1 - odd) * k
         table = legendre[index]
         scaled = (table.astype(f32) * degree_ref[...]).astype(bf16)
-        value = lax.dot_general(
-            table, scaled, (((0,), (0,)), ((), ())), preferred_element_type=f32
-        )
-        value = value * jnp.where((me == 0) & (index == 0), 0.5, 1.0).astype(f32)
-        return (value * (quad_ref[...] / lat_total)).astype(bf16)
-
-    @pl.loop(0, count // 2)
-    def _(k):
-        which, spot = k // 2, k % 2
-        first, second = operator(2 * k), operator(2 * k + 1)
-        op_send[which, 2 * spot] = first[:, 0:128]
-        op_send[which, 2 * spot + 1] = second[:, 0:128]
-        tail = jnp.concatenate([first[:, 128:lat_total], second[:, 128:lat_total]], axis=1)
-        op_send[which, 4 + spot, :, 0 : 2 * edge] = tail
-
-        @pl.when(k == 0)
-        def _():
-            op_lone[0] = first[:, 0:128]
-            op_lone[1, :, 0 : 2 * edge] = tail
-
+        return across(table, scaled) * jnp.where((me == 0) & (index == 0), 0.5, 1.0).astype(f32)
+
+    @pl.loop(0, 4)
+    def _(which):
+        tails, marks = [], []
+        for spot in range(2):
+            first, second = operator(4 * which + 2 * spot), operator(4 * which + 2 * spot + 1)
+            square = jnp.where(upper, first, second).astype(bf16)
+            op_send[which, spot * lat_total : (spot + 1) * lat_total] = square[:, 0:128]
+            tails.append(square[:, 128:lat_total])
+            line = jnp.sum(jnp.where(diagonal, second, 0.0), axis=0, keepdims=True)
+            marks.append(line[:, 0:128])
+            marks.append(
+                jnp.concatenate([line[:, 128:lat_total], jnp.zeros((1, 128 - edge), f32)], axis=1)
+            )
+
+            @pl.when(which == kind)
+            def _():
+                op_own[2 * spot] = first.astype(bf16)
+                op_own[2 * spot + 1] = second.astype(bf16)
+
+            if spot == 0:
+
+                @pl.when(which == 0)
+                def _():
+                    op_lone[0] = first[:, 0:128].astype(bf16)
+                    op_lone[1, :, 0:edge] = first[:, 128:lat_total].astype(bf16)
+
+        op_send[which, 2 * lat_total : 3 * lat_total, 0 : 2 * edge] = jnp.concatenate(tails, axis=1)
+        at = lax.broadcasted_iota(jnp.int32, (16, 128), 0)
+        lines = jnp.zeros((16, 128), f32)
+        for i in range(4):
+            lines = jnp.where(at == i, marks[i], lines)
+        op_send[which, 3 * lat_total : 3 * lat_total + 16] = lines.astype(bf16)
+
+    pl.semaphore_wait(barrier, devices - 1)
     spot_of = odd * (group - 1 - place) + (1 - odd) * place
     op_moves = []
-    for shift, other in ((1, kind + 1 - 2 * odd), (2, (kind + 2) % 4), (3, 3 - kind)):
+    for shift, other in ((2, (kind + 2) % 4), (3, 3 - kind), (1, kind + 1 - 2 * odd)):
         other_odd = other % 2
         there = other * group + other_odd * (group - 1 - spot_of) + (1 - other_odd) * spot_of
         move = remote(
@@ -721,6 +580,207 @@
     @pl.when(odd == 1)
     def _():
         lone_move.start()
+
+    loads["sea"].wait()
+
+    @pl.loop(0, rows)
+    def _(i):
+        flux = across(sea[i], to_air_ref[...])
+        flux = (flux * wet_full[i][:, 0 : flux.shape[1]]).astype(bf16)
+        flux_out[0, 0, i] = flux[0:lon_dev]
+        flux_out[0, 1, i] = flux[lon_dev : 2 * lon_dev]
+
+    partner = (lat, lon, 1 - comp)
+    moves = []
+    for part in range(2):
+        moves.append(
+            remote(flux_out.at[part, 1 - comp], flux_in.at[part, comp], flux_sem, part, partner)
+        )
+    moves[0].start()
+    loads["air"].wait()
+
+    @pl.loop(0, rows // 2)
+    def _(i):
+        for half in range(2):
+            block_of = air[pl.ds(half * rows + 2 * i, 2)].reshape(2 * lon_dev, width)
+            flux = across(block_of, to_sea_ref[...]).astype(bf16)
+            flux_out[1, half, 2 * i] = flux[0:lon_dev]
+            flux_out[1, half, 2 * i + 1] = flux[lon_dev : 2 * lon_dev]
+
+    moves[1].start()
+    kept = []
+    for part in range(2):
+        kept.append(
+            pltpu.make_async_copy(
+                flux_out.at[part, comp], flux_in.at[part, comp], local_sem.at[part]
+            )
+        )
+        kept[-1].start()
+    for name in (
+        "waves", "sea_up", "sea_down", "real", "imag", "back", "up", "down"
+    ):
+        loads[name].start()
+    for move in kept:
+        move.wait()
+    moves[0].wait()
+
+
+    def column_moves(p):
+        found = []
+        for k in range(1, col_count):
+            other = (col + k) % col_count
+            found.append(
+                remote(
+                    normed.at[p, other],
+                    columns.at[p, col],
+                    column_sem,
+                    (p, k - 1),
+                    (lat, other // 2, other % 2),
+                )
+            )
+        own = pltpu.make_async_copy(normed.at[p, col], columns.at[p, col], column_own.at[p])
+        return found + [own]
+
+    half_block = 2 * lon_dev
+    for p in range(pairs):
+
+        @pl.loop(0, col_count // 2)
+        def _(jj):
+            for j2 in range(2):
+                j = 2 * jj + j2
+                row = band * j + 2 * p
+                flux = flux_in[0, row // rows, pl.ds(row % rows, 2)].reshape(half_block, -1)
+                value = air[pl.ds(row, 2)].reshape(half_block, width).astype(f32)
+                value = value + jnp.dot(flux, from_sea_ref[...], preferred_element_type=f32)
+                forced[p, j] = value.reshape(2, lon_dev, width)
+                value = layer_norm(value, gain_ref[0:1]).astype(bf16)
+                normed[p, j] = value.reshape(2, lon_dev, width)
+
+        for move in column_moves(p):
+            move.start()
+
+    moves[1].wait()
+
+    @pl.loop(0, rows)
+    def _(i):
+        flux = jnp.concatenate([flux_in[1, 0, i], flux_in[1, 1, i]], axis=0)
+        added = jnp.dot(flux, from_air_ref[...], preferred_element_type=f32)
+        mask = wet_full[i]
+        mask = jnp.concatenate([mask, mask], axis=1)
+        field[0, i] = (sea[i].astype(f32) + mask * added).astype(bf16)
+
+    half_reach = reach // 2
+
+    def pack_strips(k):
+        @pl.loop(0, rows // 2)
+        def _(i):
+            found = []
+            for which in range(2):
+                low = field[k, 2 * i + which, 0:16].astype(f32)
+                high = field[k, 2 * i + which, cols - 16 : cols].astype(f32)
+                found.append(jnp.where(lon == 0, high[8:16], low[0:8]))
+            strips[k, i] = jnp.concatenate(found, axis=0).astype(bf16)
+
+    def halo_moves(k):
+        source, strip = field.at[k], strips.at[k]
+        low, high = pl.ds(0, reach), pl.ds(rows - reach, reach)
+        sems = halo_sem.at[k]
+        side = remote(
+            strip, sides.at[k, pl.ds(half_reach, rows // 2)], sems, 0, at_tile(tile, 1 - lon)
+        )
+        back = (
+            remote(source.at[low], edges.at[k, 1], sems, 1, at_tile(tile - 1, lon)),
+            remote(
+                strip.at[pl.ds(0, half_reach)],
+                sides.at[k, pl.ds(half_reach + rows // 2, half_reach)],
+                sems,
+                2,
+                at_tile(tile - 1, 1 - lon),
+            ),
+        )
+        ahead = (
+            remote(source.at[high], edges.at[k, 0], sems, 3, at_tile(tile + 1, lon)),
+            remote(
+                strip.at[pl.ds(rows // 2 - half_reach, half_reach)],
+                sides.at[k, pl.ds(0, half_reach)],
+                sems,
+                4,
+                at_tile(tile + 1, 1 - lon),
+            ),
+        )
+        return side, back, ahead
+
+    def send_halo(k):
+        pack_strips(k)
+        side, back, ahead = halo_moves(k)
+
+        @pl.when(tile > 0)
+        def _():
+            for move in back:
+                move.start()
+
+        @pl.when(tile < tiles - 1)
+        def _():
+            for move in ahead:
+                move.start()
+
+        side.start()
+
+    def take_halo(k):
+        @pl.loop(0, rows)
+        def _(i):
+            wide[reach + i, 8 : cols + 8] = field[k, i].astype(f32)
+
+        side, back, ahead = halo_moves(k)
+        side.wait()
+
+        @pl.when(tile > 0)
+        def _():
+            for move in back:
+                move.wait_send()
+            for move in ahead:
+                move.wait_recv()
+
+        @pl.when(tile < tiles - 1)
+        def _():
+            for move in ahead:
+                move.wait_send()
+            for move in back:
+                move.wait_recv()
+
+        def margins(first, pair, values):
+            for which in range(2):
+                part = values[8 * which : 8 * which + 8]
+                wide[first + 2 * pair + which, 0:8] = jnp.where(lon == 1, part, 0.0)
+                wide[first + 2 * pair + which, cols + 8 : cols + 16] = jnp.where(
+                    lon == 0, part, 0.0
+                )
+
+        @pl.loop(0, rows // 2)
+        def _(i):
+            margins(reach, i, sides[k, half_reach + i].astype(f32))
+
+        for which in range(2):
+            first = which * (reach + rows)
+            present = tile > 0 if which == 0 else tile < tiles - 1
+
+            @pl.when(present)
+            def _():
+                @pl.loop(0, reach)
+                def _(i):
+                    wide[first + i, 8 : cols + 8] = edges[k, which, i].astype(f32)
+
+                @pl.loop(0, half_reach)
+                def _(i):
+                    margins(first, i, sides[k, first // 2 + i].astype(f32))
+
+            @pl.when(jnp.logical_not(present))
+            def _():
+                @pl.loop(0, reach)
+                def _(i):
+                    wide[first + i] = jnp.zeros(wide.shape[1:], f32)
+
+    send_halo(0)
 
     def sea_pairs(k, first, last):
         @pl.loop(first, last)
@@ -758,43 +818,50 @@
                     mask = jnp.concatenate([mask, mask], axis=1)
                     sea_out[row] = jnp.where(mask > 0.5, value, sea[row])
 
+    def exchange(source, target, sems, own_sems):
+        def away(p, k):
+            other = (me + k) % devices
+            return remote(
+                source.at[p, other], target.at[p, me], sems, (p, k), at_device(other)
+            )
+
+        def own(p):
+            return pltpu.make_async_copy(source.at[p, me], target.at[p, me], own_sems.at[p])
+
+        def start(p):
+            @pl.loop(1, devices)
+            def _(k):
+                away(p, k).start()
+
+            own(p).start()
+
+        def wait(p):
+            own(p).wait()
+
+            @pl.loop(1, devices)
+            def _(k):
+                away(p, k).wait()
+
+        return start, wait
+
+    start_owner, wait_owner = exchange(spec_send, gathered, owner_sem, owner_own)
+    loads["waves"].wait()
+
+    for p in range(pairs):
+        for move in column_moves(p):
+            move.wait()
+        found = []
+        for which in range(2):
+            lines = jnp.concatenate([columns[p, b, which] for b in range(col_count)], axis=0)
+            value = jnp.dot(waves[...], lines, preferred_element_type=f32)
+            found.append(value.reshape(devices, 8, width))
+        spec_send[p] = jnp.concatenate(found, axis=1).astype(bf16)
+        start_owner(p)
+
     take_halo(0)
     loads["sea_up"].wait()
     loads["sea_down"].wait()
-    sea_pairs(0, 0, 2)
-
-    loads["waves"].wait()
-    own_columns.wait()
-    for move in to_columns:
-        move.wait()
-
-    def transform(t):
-        lines = jnp.concatenate([columns[b, t] for b in range(col_count)], axis=0)
-        value = jnp.dot(waves[...], lines, preferred_element_type=f32)
-        return value.reshape(devices, 8, width)
-
-    @pl.loop(0, pairs)
-    def _(p):
-        joined = jnp.concatenate([transform(2 * p), transform(2 * p + 1)], axis=1)
-        spec_send[:, p] = joined.astype(bf16)
-
-    def exchange(source, target, sems):
-        def move(k):
-            other = (me + k) % devices
-            return remote(source.at[other], target.at[me], sems, k, at_device(other))
-
-        return move
-
-    to_owner = exchange(spec_send, gathered, owner_sem)
-
-    @pl.loop(1, devices)
-    def _(k):
-        to_owner(k).start()
-
-    own = pltpu.make_async_copy(spec_send.at[me], gathered.at[me], local_sem.at[1])
-    own.start()
-
-    sea_pairs(0, 2, rows // 2)
+    sea_pairs(0, 0, rows // 2)
     send_halo(1)
 
     for move in op_moves:
@@ -807,148 +874,162 @@
     @pl.when(kind == 0)
     def _():
         for which in range(2):
-            remote(
-                op_lone, op_lone_recv.at[which], op_sem, 3 + which, at_device(me)
-            ).wait_recv()
-            op_recv[2 * which, 0] = op_lone_recv[which, 0]
-            op_recv[2 * which, 4, :, 0:edge] = op_lone_recv[which, 1, :, 0:edge]
-
-    for s in range(slots):
-        lone = (me == 0) & (s == 0)
-        for piece in range(2):
-            if piece == 0:
-                into = slice(0, 128)
-
-                def part_of(ref):
-                    return ref[s].astype(f32)
-
-            else:
-                into = slice(128, lat_total)
-
-                def part_of(ref):
-                    lanes = slice(s % 2 * edge, (s % 2 + 1) * edge)
-                    return ref[4 + s // 2, :, lanes].astype(f32)
-
-            same = part_of(op_send.at[kind]) + part_of(op_recv.at[1])
-            other = part_of(op_recv.at[0]) + part_of(op_recv.at[2])
+            remote(op_lone, op_lone_recv.at[which], op_sem, 3 + which, at_device(me)).wait_recv()
+
+    pair_at, rest_at = row_at // (2 * devices), row_at % (2 * devices)
+    source_at = band * (rest_at % devices) + 2 * pair_at + rest_at // devices
+    order = jnp.where(lane_at == source_at, 1.0, 0.0).astype(bf16)
+    unit = jnp.where(diagonal, 1.0, 0.0).astype(bf16)
+
+    def unpack(which, spot):
+        lanes = slice(spot * edge, (spot + 1) * edge)
+        square = jnp.concatenate(
+            [
+                op_recv[which, spot * lat_total : (spot + 1) * lat_total],
+                op_recv[which, 2 * lat_total : 3 * lat_total, lanes],
+            ],
+            axis=1,
+        )
+        flipped = across(unit, square)
+        square = square.astype(f32)
+        lines = op_recv[which, 3 * lat_total : 3 * lat_total + 16].astype(f32)
+        line = jnp.concatenate(
+            [lines[2 * spot : 2 * spot + 1], lines[2 * spot + 1 : 2 * spot + 2, 0:edge]], axis=1
+        )
+        first = jnp.where(upper, square, flipped)
+        second = jnp.where(upper, jnp.where(diagonal, line, flipped), square)
+        return first, second
+
+    def lone_operator(which):
+        return jnp.concatenate(
+            [op_lone_recv[which, 0], op_lone_recv[which, 1, :, 0:edge]], axis=1
+        ).astype(f32)
+
+    scale = 2.0 / lat_total * quad_ref[...]
+    for spot in range(2):
+        near, middle, far = unpack(0, spot), unpack(1, spot), unpack(2, spot)
+        for i in range(2):
+            s = 2 * spot + i
+            lone = (me == 0) & (s == 0)
+            one, three = near[i], far[i]
+            if s == 0:
+                one = jnp.where(kind == 0, lone_operator(0), one)
+                three = jnp.where(kind == 0, lone_operator(1), three)
+            same = op_own[s].astype(f32) + middle[i]
+            other = one + three
             direct = jnp.where(odd == 0, same, other)
             mirror = jnp.where(odd == 0, other, same)
-            total = jnp.where(lone, direct, direct + mirror)
-            rest = jnp.where(lone, mirror, direct + mirror)
-            skew = jnp.where(lone, 0.0, direct - mirror)
-            both[s, 0, :, into] = (2.0 * total).astype(bf16)
-            both[s, 1, :, into] = (2.0 * rest).astype(bf16)
-            gap[s, :, into] = (2.0 * skew).astype(bf16)
+
+            def ordered(value):
+                value = (value * scale).astype(bf16)
+                value = jnp.dot(order, value, preferred_element_type=f32).astype(bf16)
+                return across(value, order).astype(bf16)
+
+            both[s, 0] = ordered(jnp.where(lone, direct, direct + mirror))
+            both[s, 1] = ordered(jnp.where(lone, mirror, direct + mirror))
+            gap[s] = ordered(jnp.where(lone, 0.0, direct - mirror))
 
     loads["real"].wait()
     loads["imag"].wait()
-    own.wait()
-
-    @pl.loop(1, devices)
-    def _(k):
-        to_owner(k).wait()
-
-    chunk = devices // 8
-    lines = chunk * band * 8
-
-    @pl.loop(0, 8)
-    def _(i):
-        value = gathered[pl.ds(i * chunk, chunk)].astype(f32).reshape(lines, width)
-        for c in range(width // 128):
-            flat[c, pl.ds(i * lines, lines), :] = value[:, c * 128 : (c + 1) * 128]
-
-    def take_rows(q):
-        taken = [
-            flat[c, pl.ds(q, lat_total, stride=8), :] for c in range(width // 128)
-        ]
-        return jnp.concatenate(taken, axis=1).astype(bf16)
-
-    def put_rows(q, value):
-        for c in range(width // 128):
-            flat[c, pl.ds(q, lat_total, stride=8), :] = value[:, c * 128 : (c + 1) * 128]
+
+    lane_parts = width // 128
+    bunch = 2 * devices
+    for p in range(pairs):
+        wait_owner(p)
+        value = gathered[p].astype(f32).reshape(16 * devices, width)
+        for c in range(lane_parts):
+            flat[p, c] = value[:, c * 128 : (c + 1) * 128]
+        for q in range(8):
+            for which in range(2):
+                taken = [
+                    flat[p, c, pl.ds(8 * which + q, devices, stride=16), :]
+                    for c in range(lane_parts)
+                ]
+                at = q * bunch + which * devices
+                turned_rows[at : at + devices] = jnp.concatenate(taken, axis=1).astype(bf16)
+        for target, matrix in ((mixed_real, spec_real), (mixed_imag, spec_imag)):
+            value = jnp.dot(turned_rows[...], matrix[...], preferred_element_type=f32)
+            target[:, p * bunch : (p + 1) * bunch] = value.astype(bf16).reshape(8, bunch, width)
+
+
+    def act(matrix, value):
+        return jnp.dot(matrix, value, preferred_element_type=f32)
 
     for s in range(slots):
-        re, im = take_rows(2 * s), take_rows(2 * s + 1)
-
-        def mix(value, matrix):
-            return jnp.dot(value, matrix[...], preferred_element_type=f32).astype(bf16)
-
-        def act(matrix, value):
-            return jnp.dot(matrix, value, preferred_element_type=f32)
-
-        cosine = act(both[s, 0], mix(re, spec_real)) - act(gap[s], mix(im, spec_imag))
-        sine = act(gap[s], mix(re, spec_imag)) + act(both[s, 1], mix(im, spec_real))
-        put_rows(2 * s, cosine)
-        put_rows(2 * s + 1, sine)
-
-    @pl.loop(0, 8)
-    def _(i):
-        value = [flat[c, pl.ds(i * lines, lines), :] for c in range(width // 128)]
-        value = jnp.concatenate(value, axis=1).astype(bf16)
-        gathered[pl.ds(i * chunk, chunk)] = value.reshape(chunk, pairs, 16, width)
-
-    from_owner = exchange(gathered, returned, back_sem)
-
-    @pl.loop(1, devices)
-    def _(k):
-        from_owner(k).start()
-
-    own = pltpu.make_async_copy(gathered.at[me], returned.at[me], local_sem.at[0])
-    own.start()
+        re, im = 2 * s, 2 * s + 1
+        cosine = act(both[s, 0], mixed_real[re]) - act(gap[s], mixed_imag[im])
+        sine = act(gap[s], mixed_imag[re]) + act(both[s, 1], mixed_real[im])
+        for q, value in ((re, cosine), (im, sine)):
+            for p in range(pairs):
+                for which in range(2):
+                    at = p * bunch + which * devices
+                    for c in range(lane_parts):
+                        flat[p, c, pl.ds(8 * which + q, devices, stride=16), :] = value[
+                            at : at + devices, c * 128 : (c + 1) * 128
+                        ]
+
+    start_back, wait_back = exchange(filtered, returned, back_sem, back_own)
+    for p in range(pairs):
+        value = jnp.concatenate([flat[p, c] for c in range(lane_parts)], axis=1)
+        filtered[p] = value.astype(bf16).reshape(devices, 16, width)
+        start_back(p)
 
     take_halo(1)
     sea_pairs(1, 0, rows // 2)
 
-    loads["back"].wait()
-    own.wait()
-
-    @pl.loop(1, devices)
-    def _(k):
-        from_owner(k).wait()
-
-    @pl.loop(0, pairs)
-    def _(p):
-        value = returned[:, p].astype(f32)
+    def grid_moves(p):
+        found = []
+        for k in range(1, col_count):
+            other = (col + k) % col_count
+            found.append(
+                remote(
+                    spatial.at[p, other],
+                    spectral.at[p, col],
+                    grid_sem,
+                    (p, k - 1),
+                    (lat, other // 2, other % 2),
+                )
+            )
+        own = pltpu.make_async_copy(spatial.at[p, col], spectral.at[p, col], grid_own.at[p])
+        return found + [own]
+
+    def to_grid(p):
+        wait_back(p)
+        value = returned[p].astype(f32)
         for which in range(2):
             lines = value[:, 8 * which : 8 * which + 8].reshape(circle, width).astype(bf16)
             line = jnp.dot(waves_back[...], lines, preferred_element_type=f32).astype(bf16)
             for b in range(col_count):
-                spatial[b, 2 * p + which] = line[b * lon_dev : (b + 1) * lon_dev]
-
-    to_grid = []
-    for k in range(1, col_count):
-        other = (col + k) % col_count
-        move = remote(
-            spatial.at[other],
-            spectral.at[pl.ds(col * band, band)],
-            grid_sem,
-            k - 1,
-            (lat, other // 2, other % 2),
-        )
-        move.start()
-        to_grid.append(move)
-    own = pltpu.make_async_copy(
-        spatial.at[col], spectral.at[pl.ds(col * band, band)], local_sem.at[1]
-    )
-    own.start()
-
+                spatial[p, b, which] = line[b * lon_dev : (b + 1) * lon_dev]
+        for move in grid_moves(p):
+            move.start()
+
+    def finish(p):
+        for move in grid_moves(p):
+            move.wait()
+
+        @pl.loop(0, col_count // 2)
+        def _(jj):
+            here = pl.ds(2 * jj, 2)
+            value = forced[p, here].reshape(2 * half_block, width)
+            value = value + spectral[p, here].reshape(2 * half_block, width).astype(f32)
+            inner = layer_norm(value, gain_ref[1:2]).astype(bf16)
+            hidden = jax.nn.gelu(
+                jnp.dot(inner, air_up[...], preferred_element_type=f32)
+            ).astype(bf16)
+            value = value + jnp.dot(hidden, air_down[...], preferred_element_type=f32)
+            value = value.astype(bf16).reshape(2, 2, lon_dev, width)
+            for j2 in range(2):
+                air_out[pl.ds(band * (2 * jj + j2) + 2 * p, 2)] = value[j2]
+
+    loads["back"].wait()
     loads["up"].wait()
     loads["down"].wait()
-    own.wait()
-    for move in to_grid:
-        move.wait()
-
-    @pl.loop(0, lat_dev // per)
-    def _(i):
-        here = pl.ds(i * per, per)
-        mixed = forced[here].reshape(block, width)
-        mixed = mixed + spectral[here].reshape(block, width).astype(f32)
-        value = layer_norm(mixed, gain_ref[1:2]).astype(bf16)
-        hidden = jax.nn.gelu(
-            jnp.dot(value, air_up[...], preferred_element_type=f32)
-        ).astype(bf16)
-        mixed = mixed + jnp.dot(hidden, air_down[...], preferred_element_type=f32)
-        air_out[here] = mixed.astype(bf16).reshape(per, lon_dev, width)
+    for p in range(pairs):
+        to_grid(p)
+        if p > 0:
+            finish(p - 1)
+    finish(pairs - 1)
 
 
 def whole_step(
@@ -989,8 +1070,9 @@
     waves_back = jnp.asarray(table.T, f32).astype(bf16)
     vmem = pl.BlockSpec(memory_space=pltpu.VMEM)
     hbm = pl.BlockSpec(memory_space=pl.ANY)
-    tall = (devices, band // 2, 16, width)
-    squares = (lat_total, 128)
+    pairs = band // 2
+    tall = (pairs, devices, 16, width)
+    patches = (pairs, col_count, 2, lon_dev, width)
     dma = pltpu.SemaphoreType.DMA
     return pl.pallas_call(
         functools.partial(whole_step_body, lat_total),
@@ -1006,7 +1088,7 @@
         scratch_shapes=[
             pltpu.VMEM(atm_state.shape, bf16),
             pltpu.VMEM(ocean_state.shape, bf16),
-            pltpu.VMEM(legendre.shape, bf16),
+            pltpu.VMEM((legendre.shape[0], lat_total, legendre.shape[1]), bf16),
             pltpu.VMEM(spec_real.shape, bf16),
             pltpu.VMEM(spec_imag.shape, bf16),
             pltpu.VMEM(atm_up.shape, bf16),
@@ -1020,33 +1102,43 @@
             pltpu.VMEM((rows, cols, 128), f32),
             pltpu.VMEM((2, 2, rows, lon_dev, surface), bf16),
             pltpu.VMEM((2, 2, rows, lon_dev, surface), bf16),
-            pltpu.VMEM(atm_state.shape, f32),
-            pltpu.VMEM(atm_state.shape, bf16),
-            pltpu.VMEM((col_count, band, lon_dev, width), bf16),
+            pltpu.VMEM(patches, f32),
+            pltpu.VMEM(patches, bf16),
+            pltpu.VMEM(patches, bf16),
             pltpu.VMEM(tall, bf16),
             pltpu.VMEM(tall, bf16),
-            pltpu.VMEM((width // 128, devices * band * 8, 128), f32),
+            pltpu.VMEM((pairs, width // 128, 16 * devices, 128), f32),
+            pltpu.VMEM((16 * devices, width), bf16),
+            pltpu.VMEM((8, lat_total, width), bf16),
+            pltpu.VMEM((8, lat_total, width), bf16),
             pltpu.VMEM(tall, bf16),
-            pltpu.VMEM((col_count, band, lon_dev, width), bf16),
-            pltpu.VMEM(atm_state.shape, bf16),
-            pltpu.VMEM((4, 6) + squares, bf16),
-            pltpu.VMEM((3, 6) + squares, bf16),
-            pltpu.VMEM((2,) + squares, bf16),
-            pltpu.VMEM((2, 2) + squares, bf16),
+            pltpu.VMEM(tall, bf16),
+            pltpu.VMEM(patches, bf16),
+            pltpu.VMEM(patches, bf16),
+            pltpu.VMEM((4, 3 * lat_total + 16, 128), bf16),
+            pltpu.VMEM((3, 3 * lat_total + 16, 128), bf16),
+            pltpu.VMEM((slots, lat_total, lat_total), bf16),
+            pltpu.VMEM((2, lat_total, 128), bf16),
+            pltpu.VMEM((2, 2, lat_total, 128), bf16),
             pltpu.VMEM((slots, 2, lat_total, lat_total), bf16),
             pltpu.VMEM((slots, lat_total, lat_total), bf16),
             pltpu.VMEM((2,) + ocean_state.shape, bf16),
             pltpu.VMEM((2, 2, reach, cols, sea_width), bf16),
-            pltpu.VMEM((2, rows + 2 * reach, 16, sea_width), bf16),
+            pltpu.VMEM((2, rows // 2, 16, sea_width), bf16),
+            pltpu.VMEM((2, rows // 2 + reach, 16, sea_width), bf16),
             pltpu.VMEM((rows + 2 * reach, cols + 16, sea_width), f32),
             pltpu.VMEM((2 * cols, sea_width), f32),
             dma((11,)),
             dma((2,)),
             dma((2, 2)),
-            dma((2, 3)),
-            dma((2, devices)),
-            dma((2, devices)),
-            dma((2, 3)),
+            dma((2, pairs, 3)),
+            dma((pairs,)),
+            dma((2, pairs, devices)),
+            dma((pairs,)),
+            dma((2, pairs, devices)),
+            dma((pairs,)),
+            dma((2, pairs, 3)),
+            dma((pairs,)),
             dma((2, 5)),
             dma((2, 2, 5)),
         ],
@@ -1057,19 +1149,19 @@
         atm_state,
         ocean_state,
         wet_mask,
-        legendre,
+        jnp.swapaxes(legendre, 1, 2),
         quad_weight[None, :],
         spec_real,
         spec_imag,
-        degree_gain[:, None],
+        degree_gain[None, :],
         atm_gain,
         atm_up,
         atm_down,
-        atm_to_surface,
+        atm_to_surface.T,
         surface_to_atm,
-        ocean_to_surface,
+        ocean_to_surface.T,
         surface_to_ocean,
-        ocean_kernel,
+        ocean_kernel.transpose(1, 2, 0, 3),
         ocean_gain,
         ocean_up,
         ocean_down,

time: 145 us -> 122 us (0.84)
  Pallas kernels: 130 us -> 116 us
  local copies, waits for them, and re-layouts: 13.7 us -> 4.61 us
    pallas_call x1, Pallas kernels: 130 us -> 116 us  [whole_step(): pl.pallas_call(functools.partial(whole_step_body, lat_total), out_shape=(...]
    unnamed x8 -> x4, local copies, waits for them, and re-layouts: 12.2 us -> 3.36 us
where the time goes in v1:
time: 122 us; the launch traced here: 121 us
  Pallas kernels  116 us (95%)
  local copies, waits for them, and re-layouts  4.61 us (4%)
    pallas_call x1, Pallas kernels, whole_step(): pl.pallas_call(functools.partial(whole_step_body, lat_total), out_shape=(...  116 us
    unnamed x4, local copies, waits for them, and re-layouts  3.36 us

profile of v1, /device:TPU:13, one launch (start us, length us, event | category | flops | bytes accessed | tf_op | source)
XLA Modules:
  0.0 121.3 jit_solution(1667526055211298570)
XLA Ops:
  0.6 1.2 %broadcast_in_dim.7.degree_ref = f32[1,384]{1,0:T(1,128)} reshape(f32[384]{0:T(512)} %param.28) | data formatting | bytes 3072 | tf_op jit(solution)/shard_map/broadcast_in_dim | solution.py:1156
  1.9 116.0 %shard_map.212 = (bf16[24,64,384]{2,1,0:T(8,128)(2,1)}, bf16[12,128,256]{2,1,0:T(8,128)(2,1)}) custom-call(bf16[24,64,384]{2,1,0:T(8,128)(2,1)} %atm_hbm.1, bf16[12,128,256]{2,1,0:T(8,128)(2,1)} %sea_hbm.1, s32[12,128]{1,0:T(8,128)} %wet_ref.1, bf16[16,192,384]{2,1,0:T(8,128)(2,1)} %bitcast.5, f32[1,192]{1,0:T(1,128)} %bitcast.9, bf16[384,384]{1,0:T(8,128)(2,1)} %real_hbm.1, ...), custom_call_target="tpu_custom_call" | custom-call | tf_op jit(solution)/shard_map/pallas_call | solution.py:1077
  117.9 0.0 copy-start
  117.9 2.5 %copy.25 = bf16[24,64,384]{2,1,0:T(8,128)(2,1)} copy(bf16[24,64,384]{2,1,0:T(8,128)(2,1)} %get-tuple-element.4) | data formatting | bytes 2359296
  120.4 0.0 copy-done
  120.4 0.9 copy.26
Async XLA Ops:
  117.9 2.5 %copy-start = (bf16[12,128,256]{2,1,0:T(8,128)(2,1)S(1)}, bf16[12,128,256]{2,1,0:T(8,128)(2,1)}, u32[]{:S(2)}) copy-start(bf16[12,128,256]{2,1,0:T(8,128)(2,1)} %get-tuple-element.5) | copy-start | bytes 2359300

commit v2 on v1

--- a/solution.py
+++ b/solution.py
@@ -337,11 +337,12 @@
         and lax.axis_size("comp") == 2
         and circle // devices == 8
         and legendre.shape[0] == 16
-        and lat_dev // col_count % 2 == 0
+        and lat_dev // col_count == 6
         and lat_dev == 2 * rows
         and cols == 2 * lon_dev
         and cols == 128
         and rows == 2 * reach
+        and rows % 6 == 0
         and reach % 2 == 0
         and rows % (2 * OCEAN_DILATION) == 0
         and 128 < legendre.shape[2] <= 192
@@ -408,15 +409,16 @@
     spectral,
     op_send,
     op_recv,
-    op_own,
+    op_sum,
+    op_other,
     op_lone,
-    op_lone_recv,
     both,
     gap,
     field,
     edges,
     strips,
     sides,
+    corners,
     wide,
     stencil,
     load_sem,
@@ -526,69 +528,96 @@
     def operator(k):
         index = odd * ((count - k) % count) + (1 - odd) * k
         table = legendre[index]
-        scaled = (table.astype(f32) * degree_ref[...]).astype(bf16)
+        scaled = (table.astype(f32) * degree_ref[...][None, :]).astype(bf16)
         return across(table, scaled) * jnp.where((me == 0) & (index == 0), 0.5, 1.0).astype(f32)
 
-    @pl.loop(0, 4)
-    def _(which):
-        tails, marks = [], []
-        for spot in range(2):
-            first, second = operator(4 * which + 2 * spot), operator(4 * which + 2 * spot + 1)
-            square = jnp.where(upper, first, second).astype(bf16)
-            op_send[which, spot * lat_total : (spot + 1) * lat_total] = square[:, 0:128]
-            tails.append(square[:, 128:lat_total])
-            line = jnp.sum(jnp.where(diagonal, second, 0.0), axis=0, keepdims=True)
-            marks.append(line[:, 0:128])
-            marks.append(
-                jnp.concatenate([line[:, 128:lat_total], jnp.zeros((1, 128 - edge), f32)], axis=1)
+    high_half = kind // 2
+
+    def fill_operators(first_group):
+        @pl.loop(first_group, first_group + 2)
+        def _(which):
+            tails, marks = [], []
+            for spot in range(2):
+                first, second = operator(4 * which + 2 * spot), operator(4 * which + 2 * spot + 1)
+                square = jnp.where(upper, first, second).astype(bf16)
+                op_send[which, spot * lat_total : (spot + 1) * lat_total] = square[:, 0:128]
+                tails.append(square[:, 128:lat_total])
+                line = jnp.sum(jnp.where(diagonal, second, 0.0), axis=0, keepdims=True)
+                marks.append(line[:, 0:128])
+                marks.append(
+                    jnp.concatenate(
+                        [line[:, 128:lat_total], jnp.zeros((1, 128 - edge), f32)], axis=1
+                    )
+                )
+
+            op_send[which, 2 * lat_total : 3 * lat_total, 0 : 2 * edge] = jnp.concatenate(
+                tails, axis=1
             )
-
-            @pl.when(which == kind)
-            def _():
-                op_own[2 * spot] = first.astype(bf16)
-                op_own[2 * spot + 1] = second.astype(bf16)
-
-            if spot == 0:
-
-                @pl.when(which == 0)
-                def _():
-                    op_lone[0] = first[:, 0:128].astype(bf16)
-                    op_lone[1, :, 0:edge] = first[:, 128:lat_total].astype(bf16)
-
-        op_send[which, 2 * lat_total : 3 * lat_total, 0 : 2 * edge] = jnp.concatenate(tails, axis=1)
-        at = lax.broadcasted_iota(jnp.int32, (16, 128), 0)
-        lines = jnp.zeros((16, 128), f32)
-        for i in range(4):
-            lines = jnp.where(at == i, marks[i], lines)
-        op_send[which, 3 * lat_total : 3 * lat_total + 16] = lines.astype(bf16)
-
+            at = lax.broadcasted_iota(jnp.int32, (16, 128), 0)
+            lines = jnp.zeros((16, 128), f32)
+            for i in range(4):
+                lines = jnp.where(at == i, marks[i], lines)
+            op_send[which, 3 * lat_total : 3 * lat_total + 16] = lines.astype(bf16)
+
+    fill_operators(2 * (1 - high_half))
     pl.semaphore_wait(barrier, devices - 1)
+    across_kind = (kind + 2) % 4
+    op_first = [
+        remote(
+            op_send.at[2 * (1 - high_half) + j],
+            op_recv.at[j],
+            op_sem,
+            k,
+            at_device(across_kind * group + place),
+        )
+        for k, j in enumerate((1 - odd, odd))
+    ]
+    op_first[0].start()
     spot_of = odd * (group - 1 - place) + (1 - odd) * place
-    op_moves = []
-    for shift, other in ((2, (kind + 2) % 4), (3, 3 - kind), (1, kind + 1 - 2 * odd)):
-        other_odd = other % 2
-        there = other * group + other_odd * (group - 1 - spot_of) + (1 - other_odd) * spot_of
-        move = remote(
-            op_send.at[other], op_recv.at[shift - 1], op_sem, shift - 1, at_device(there)
+    beside = kind + 1 - 2 * odd
+    beside_place = odd * spot_of + (1 - odd) * (group - 1 - spot_of)
+    op_second = remote(
+        op_sum.at[1 - odd], op_other, op_sem, 2, at_device(beside * group + beside_place)
+    )
+    lone_moves = [
+        remote(
+            op_sum.at[0, pl.ds(start, lat_total)],
+            op_lone.at[k],
+            op_sem,
+            3 + k,
+            at_device((group - place) % group),
         )
-        move.start()
-        op_moves.append(move)
-    lone_move = remote(
-        op_lone, op_lone_recv.at[kind // 2], op_sem, 3 + kind // 2, at_device((group - place) % group)
-    )
-
-    @pl.when(odd == 1)
-    def _():
-        lone_move.start()
+        for k, start in enumerate((0, 2 * lat_total))
+    ]
+
+    def sum_operators(j):
+        mine = op_send[2 * high_half + j].astype(f32)
+        op_sum[j] = (mine + op_recv[j].astype(f32)).astype(bf16)
+
+    def pass_operators():
+        op_first[0].wait()
+        sum_operators(1 - odd)
+        op_second.start()
+
+        @pl.when(kind == 1)
+        def _():
+            for move in lone_moves:
+                move.start()
+
+    def keep_operators():
+        op_first[1].wait()
+        sum_operators(odd)
 
     loads["sea"].wait()
 
-    @pl.loop(0, rows)
-    def _(i):
-        flux = across(sea[i], to_air_ref[...])
-        flux = (flux * wet_full[i][:, 0 : flux.shape[1]]).astype(bf16)
-        flux_out[0, 0, i] = flux[0:lon_dev]
-        flux_out[0, 1, i] = flux[lon_dev : 2 * lon_dev]
+    few = rows // 3
+    for part in range(3):
+        here = slice(part * few, (part + 1) * few)
+        flux = across(sea[here].reshape(few * cols, sea_width), to_air_ref[...])
+        flux = flux.reshape(few, cols, -1)
+        flux = (flux * wet_full[here, :, 0 : flux.shape[2]]).astype(bf16)
+        flux_out[0, 0, here] = flux[:, 0:lon_dev]
+        flux_out[0, 1, here] = flux[:, lon_dev : 2 * lon_dev]
 
     partner = (lat, lon, 1 - comp)
     moves = []
@@ -599,13 +628,11 @@
     moves[0].start()
     loads["air"].wait()
 
-    @pl.loop(0, rows // 2)
-    def _(i):
-        for half in range(2):
-            block_of = air[pl.ds(half * rows + 2 * i, 2)].reshape(2 * lon_dev, width)
-            flux = across(block_of, to_sea_ref[...]).astype(bf16)
-            flux_out[1, half, 2 * i] = flux[0:lon_dev]
-            flux_out[1, half, 2 * i + 1] = flux[lon_dev : 2 * lon_dev]
+    for part in range(4):
+        here = slice(part * rows // 2, (part + 1) * rows // 2)
+        there = slice(part % 2 * rows // 2, (part % 2 + 1) * rows // 2)
+        flux = across(air[here].reshape(rows // 2 * lon_dev, width), to_sea_ref[...])
+        flux_out[1, part // 2, there] = flux.astype(bf16).reshape(rows // 2, lon_dev, -1)
 
     moves[1].start()
     kept = []
@@ -670,6 +697,8 @@
         field[0, i] = (sea[i].astype(f32) + mask * added).astype(bf16)
 
     half_reach = reach // 2
+    far = tile - 1 + 2 * comp
+    has_far = (far >= 0) & (far < tiles)
 
     def pack_strips(k):
         @pl.loop(0, rows // 2)
@@ -681,133 +710,121 @@
                 found.append(jnp.where(lon == 0, high[8:16], low[0:8]))
             strips[k, i] = jnp.concatenate(found, axis=0).astype(bf16)
 
-    def halo_moves(k):
-        source, strip = field.at[k], strips.at[k]
-        low, high = pl.ds(0, reach), pl.ds(rows - reach, reach)
-        sems = halo_sem.at[k]
-        side = remote(
-            strip, sides.at[k, pl.ds(half_reach, rows // 2)], sems, 0, at_tile(tile, 1 - lon)
-        )
-        back = (
-            remote(source.at[low], edges.at[k, 1], sems, 1, at_tile(tile - 1, lon)),
+    def side_move(k):
+        return remote(strips.at[k], sides.at[k], halo_sem.at[k], 0, at_tile(tile, 1 - lon))
+
+    def edge_moves(k, which):
+        target = far if which else tile + 1 - 2 * comp
+        upper_half = comp if which else 1 - comp
+        return (
             remote(
-                strip.at[pl.ds(0, half_reach)],
-                sides.at[k, pl.ds(half_reach + rows // 2, half_reach)],
-                sems,
-                2,
-                at_tile(tile - 1, 1 - lon),
+                field.at[k, pl.ds(reach * upper_half, reach)],
+                edges.at[k, which],
+                halo_sem.at[k],
+                1 + 2 * which,
+                at_tile(target, lon),
+            ),
+            remote(
+                strips.at[k, pl.ds(half_reach * upper_half, half_reach)],
+                corners.at[k, which],
+                halo_sem.at[k],
+                2 + 2 * which,
+                at_tile(target, 1 - lon),
             ),
         )
-        ahead = (
-            remote(source.at[high], edges.at[k, 0], sems, 3, at_tile(tile + 1, lon)),
-            remote(
-                strip.at[pl.ds(rows // 2 - half_reach, half_reach)],
-                sides.at[k, pl.ds(0, half_reach)],
-                sems,
-                4,
-                at_tile(tile + 1, 1 - lon),
-            ),
-        )
-        return side, back, ahead
 
     def send_halo(k):
         pack_strips(k)
-        side, back, ahead = halo_moves(k)
-
-        @pl.when(tile > 0)
+
+        @pl.when(has_far)
         def _():
-            for move in back:
+            for move in edge_moves(k, 1):
                 move.start()
 
-        @pl.when(tile < tiles - 1)
-        def _():
-            for move in ahead:
-                move.start()
-
-        side.start()
-
-    def take_halo(k):
+        side_move(k).start()
+        for move in edge_moves(k, 0):
+            move.start()
+
+    def margins(first, pair, values):
+        for which in range(2):
+            part = values[8 * which : 8 * which + 8]
+            wide[first + 2 * pair + which, 0:8] = jnp.where(lon == 1, part, 0.0)
+            wide[first + 2 * pair + which, cols + 8 : cols + 16] = jnp.where(lon == 0, part, 0.0)
+
+    def fill_edge(k, which, first):
+        @pl.loop(0, reach)
+        def _(i):
+            wide[first + i, 8 : cols + 8] = edges[k, which, i].astype(f32)
+
+        @pl.loop(0, half_reach)
+        def _(i):
+            margins(first, i, corners[k, which, i].astype(f32))
+
+    def take_near(k):
         @pl.loop(0, rows)
         def _(i):
             wide[reach + i, 8 : cols + 8] = field[k, i].astype(f32)
 
-        side, back, ahead = halo_moves(k)
-        side.wait()
-
-        @pl.when(tile > 0)
-        def _():
-            for move in back:
-                move.wait_send()
-            for move in ahead:
-                move.wait_recv()
-
-        @pl.when(tile < tiles - 1)
-        def _():
-            for move in ahead:
-                move.wait_send()
-            for move in back:
-                move.wait_recv()
-
-        def margins(first, pair, values):
-            for which in range(2):
-                part = values[8 * which : 8 * which + 8]
-                wide[first + 2 * pair + which, 0:8] = jnp.where(lon == 1, part, 0.0)
-                wide[first + 2 * pair + which, cols + 8 : cols + 16] = jnp.where(
-                    lon == 0, part, 0.0
-                )
+        side_move(k).wait()
+        for move in edge_moves(k, 0):
+            move.wait()
 
         @pl.loop(0, rows // 2)
         def _(i):
-            margins(reach, i, sides[k, half_reach + i].astype(f32))
-
-        for which in range(2):
-            first = which * (reach + rows)
-            present = tile > 0 if which == 0 else tile < tiles - 1
-
-            @pl.when(present)
-            def _():
-                @pl.loop(0, reach)
-                def _(i):
-                    wide[first + i, 8 : cols + 8] = edges[k, which, i].astype(f32)
-
-                @pl.loop(0, half_reach)
-                def _(i):
-                    margins(first, i, sides[k, first // 2 + i].astype(f32))
-
-            @pl.when(jnp.logical_not(present))
-            def _():
-                @pl.loop(0, reach)
-                def _(i):
-                    wide[first + i] = jnp.zeros(wide.shape[1:], f32)
+            margins(reach, i, sides[k, i].astype(f32))
+
+        fill_edge(k, 0, (reach + rows) * (1 - comp))
+
+    def take_far(k):
+        first = (reach + rows) * comp
+
+        @pl.when(has_far)
+        def _():
+            for move in edge_moves(k, 1):
+                move.wait()
+            fill_edge(k, 1, first)
+
+        @pl.when(jnp.logical_not(has_far))
+        def _():
+            @pl.loop(0, reach)
+            def _(i):
+                wide[first + i] = jnp.zeros(wide.shape[1:], f32)
 
     send_halo(0)
-
-    def sea_pairs(k, first, last):
-        @pl.loop(first, last)
-        def _(pair):
-            base = pair // step * (2 * step) + pair % step
+    op_first[1].start()
+    fill_operators(2 * high_half)
+
+    triple = reach // step
+    slab = cols // 2
+
+    def sea_half(k, upper_half):
+        @pl.loop(0, step)
+        def _(parity):
+            base = upper_half * reach + parity
             for half in range(sea_width // 128):
                 part = slice(half * 128, (half + 1) * 128)
-                sums = [jnp.zeros((cols, 128), f32) for _ in range(2)]
-                for a in range(STENCIL_TAPS + 1):
-                    for b in range(STENCIL_TAPS):
-                        start = 8 - reach + b * step
-                        window = wide[base + a * step, start : start + cols, part]
-                        for which in range(2):
-                            tap = a - which
-                            if 0 <= tap < STENCIL_TAPS:
-                                weight = taps[
-                                    (k * STENCIL_TAPS + tap) * STENCIL_TAPS + b, :, part
-                                ]
-                                sums[which] = sums[which] + window * weight
-                for which in range(2):
-                    stencil[which * cols : (which + 1) * cols, part] = sums[which]
+                for side in range(2):
+                    sums = [jnp.zeros((slab, 128), f32) for _ in range(triple)]
+                    for a in range(STENCIL_TAPS + triple - 1):
+                        for b in range(STENCIL_TAPS):
+                            start = 8 - reach + b * step + side * slab
+                            window = wide[base + a * step, start : start + slab, part]
+                            for which in range(triple):
+                                tap = a - which
+                                if 0 <= tap < STENCIL_TAPS:
+                                    weight = taps[
+                                        (k * STENCIL_TAPS + tap) * STENCIL_TAPS + b, :, part
+                                    ]
+                                    sums[which] = sums[which] + window * weight
+                    for which in range(triple):
+                        at = which * cols + side * slab
+                        stencil[at : at + slab, part] = sums[which]
             values = layer_norm(stencil[...], sea_gain_ref[k : k + 1]).astype(bf16)
             hidden = jax.nn.gelu(
                 jnp.dot(values, sea_up[k], preferred_element_type=f32)
             ).astype(bf16)
             moved = jnp.dot(hidden, sea_down[k], preferred_element_type=f32)
-            for which in range(2):
+            for which in range(triple):
                 row = base + which * step
                 centre = wide[row + reach, 8 : 8 + cols, :]
                 value = (centre + moved[which * cols : (which + 1) * cols]).astype(bf16)
@@ -858,83 +875,23 @@
         spec_send[p] = jnp.concatenate(found, axis=1).astype(bf16)
         start_owner(p)
 
-    take_halo(0)
+    pass_operators()
+    take_near(0)
     loads["sea_up"].wait()
     loads["sea_down"].wait()
-    sea_pairs(0, 0, rows // 2)
+    sea_half(0, 1 - comp)
+    take_far(0)
+    sea_half(0, comp)
     send_halo(1)
-
-    for move in op_moves:
-        move.wait()
-
-    @pl.when(odd == 1)
-    def _():
-        lone_move.wait_send()
-
-    @pl.when(kind == 0)
-    def _():
-        for which in range(2):
-            remote(op_lone, op_lone_recv.at[which], op_sem, 3 + which, at_device(me)).wait_recv()
-
-    pair_at, rest_at = row_at // (2 * devices), row_at % (2 * devices)
-    source_at = band * (rest_at % devices) + 2 * pair_at + rest_at // devices
-    order = jnp.where(lane_at == source_at, 1.0, 0.0).astype(bf16)
-    unit = jnp.where(diagonal, 1.0, 0.0).astype(bf16)
-
-    def unpack(which, spot):
-        lanes = slice(spot * edge, (spot + 1) * edge)
-        square = jnp.concatenate(
-            [
-                op_recv[which, spot * lat_total : (spot + 1) * lat_total],
-                op_recv[which, 2 * lat_total : 3 * lat_total, lanes],
-            ],
-            axis=1,
-        )
-        flipped = across(unit, square)
-        square = square.astype(f32)
-        lines = op_recv[which, 3 * lat_total : 3 * lat_total + 16].astype(f32)
-        line = jnp.concatenate(
-            [lines[2 * spot : 2 * spot + 1], lines[2 * spot + 1 : 2 * spot + 2, 0:edge]], axis=1
-        )
-        first = jnp.where(upper, square, flipped)
-        second = jnp.where(upper, jnp.where(diagonal, line, flipped), square)
-        return first, second
-
-    def lone_operator(which):
-        return jnp.concatenate(
-            [op_lone_recv[which, 0], op_lone_recv[which, 1, :, 0:edge]], axis=1
-        ).astype(f32)
-
-    scale = 2.0 / lat_total * quad_ref[...]
-    for spot in range(2):
-        near, middle, far = unpack(0, spot), unpack(1, spot), unpack(2, spot)
-        for i in range(2):
-            s = 2 * spot + i
-            lone = (me == 0) & (s == 0)
-            one, three = near[i], far[i]
-            if s == 0:
-                one = jnp.where(kind == 0, lone_operator(0), one)
-                three = jnp.where(kind == 0, lone_operator(1), three)
-            same = op_own[s].astype(f32) + middle[i]
-            other = one + three
-            direct = jnp.where(odd == 0, same, other)
-            mirror = jnp.where(odd == 0, other, same)
-
-            def ordered(value):
-                value = (value * scale).astype(bf16)
-                value = jnp.dot(order, value, preferred_element_type=f32).astype(bf16)
-                return across(value, order).astype(bf16)
-
-            both[s, 0] = ordered(jnp.where(lone, direct, direct + mirror))
-            both[s, 1] = ordered(jnp.where(lone, mirror, direct + mirror))
-            gap[s] = ordered(jnp.where(lone, 0.0, direct - mirror))
+    keep_operators()
 
     loads["real"].wait()
     loads["imag"].wait()
 
     lane_parts = width // 128
     bunch = 2 * devices
-    for p in range(pairs):
+
+    def mix_rows(p):
         wait_owner(p)
         value = gathered[p].astype(f32).reshape(16 * devices, width)
         for c in range(lane_parts):
@@ -951,6 +908,69 @@
             value = jnp.dot(turned_rows[...], matrix[...], preferred_element_type=f32)
             target[:, p * bunch : (p + 1) * bunch] = value.astype(bf16).reshape(8, bunch, width)
 
+    for p in range(pairs - 1):
+        mix_rows(p)
+
+    op_second.wait()
+
+    @pl.when(kind == 1)
+    def _():
+        for move in lone_moves:
+            move.wait_send()
+
+    @pl.when(kind == 0)
+    def _():
+        for move in lone_moves:
+            move.wait_recv()
+
+    pair_at, rest_at = row_at // (2 * devices), row_at % (2 * devices)
+    source_at = band * (rest_at % devices) + 2 * pair_at + rest_at // devices
+    order = jnp.where(lane_at == source_at, 1.0, 0.0).astype(bf16)
+    unit = jnp.where(diagonal, 1.0, 0.0).astype(bf16)
+
+    def unpack(packed, spot):
+        lanes = slice(spot * edge, (spot + 1) * edge)
+        square = jnp.concatenate(
+            [
+                packed[spot * lat_total : (spot + 1) * lat_total],
+                packed[2 * lat_total : 3 * lat_total, lanes],
+            ],
+            axis=1,
+        )
+        flipped = across(unit, square)
+        square = square.astype(f32)
+        lines = packed[3 * lat_total : 3 * lat_total + 16].astype(f32)
+        line = jnp.concatenate(
+            [lines[2 * spot : 2 * spot + 1], lines[2 * spot + 1 : 2 * spot + 2, 0:edge]], axis=1
+        )
+        first = jnp.where(upper, square, flipped)
+        second = jnp.where(upper, jnp.where(diagonal, line, flipped), square)
+        return first, second
+
+    scale = 2.0 / lat_total * quad_ref[...]
+    for spot in range(2):
+        same, other = unpack(op_sum.at[odd], spot), unpack(op_other, spot)
+        for i in range(2):
+            s = 2 * spot + i
+            lone = (me == 0) & (s == 0)
+            theirs = other[i]
+            if s == 0:
+                alone = jnp.concatenate([op_lone[0], op_lone[1, :, 0:edge]], axis=1)
+                alone = jnp.where(upper, alone.astype(f32), across(unit, alone))
+                theirs = jnp.where(kind == 0, alone, theirs)
+            direct = jnp.where(odd == 0, same[i], theirs)
+            mirror = jnp.where(odd == 0, theirs, same[i])
+
+            def ordered(value):
+                value = (value * scale).astype(bf16)
+                value = jnp.dot(order, value, preferred_element_type=f32).astype(bf16)
+                return across(value, order).astype(bf16)
+
+            both[s, 0] = ordered(jnp.where(lone, direct, direct + mirror))
+            both[s, 1] = ordered(jnp.where(lone, mirror, direct + mirror))
+            gap[s] = ordered(jnp.where(lone, 0.0, direct - mirror))
+
+    mix_rows(pairs - 1)
 
     def act(matrix, value):
         return jnp.dot(matrix, value, preferred_element_type=f32)
@@ -974,8 +994,8 @@
         filtered[p] = value.astype(bf16).reshape(devices, 16, width)
         start_back(p)
 
-    take_halo(1)
-    sea_pairs(1, 0, rows // 2)
+    take_near(1)
+    sea_half(1, 1 - comp)
 
     def grid_moves(p):
         found = []
@@ -1025,11 +1045,14 @@
     loads["back"].wait()
     loads["up"].wait()
     loads["down"].wait()
-    for p in range(pairs):
-        to_grid(p)
-        if p > 0:
-            finish(p - 1)
-    finish(pairs - 1)
+    to_grid(0)
+    take_far(1)
+    sea_half(1, comp)
+    to_grid(1)
+    finish(0)
+    to_grid(2)
+    finish(1)
+    finish(2)
 
 
 def whole_step(
@@ -1116,18 +1139,19 @@
             pltpu.VMEM(patches, bf16),
             pltpu.VMEM(patches, bf16),
             pltpu.VMEM((4, 3 * lat_total + 16, 128), bf16),
-            pltpu.VMEM((3, 3 * lat_total + 16, 128), bf16),
-            pltpu.VMEM((slots, lat_total, lat_total), bf16),
+            pltpu.VMEM((2, 3 * lat_total + 16, 128), bf16),
+            pltpu.VMEM((2, 3 * lat_total + 16, 128), bf16),
+            pltpu.VMEM((3 * lat_total + 16, 128), bf16),
             pltpu.VMEM((2, lat_total, 128), bf16),
-            pltpu.VMEM((2, 2, lat_total, 128), bf16),
             pltpu.VMEM((slots, 2, lat_total, lat_total), bf16),
             pltpu.VMEM((slots, lat_total, lat_total), bf16),
             pltpu.VMEM((2,) + ocean_state.shape, bf16),
             pltpu.VMEM((2, 2, reach, cols, sea_width), bf16),
             pltpu.VMEM((2, rows // 2, 16, sea_width), bf16),
-            pltpu.VMEM((2, rows // 2 + reach, 16, sea_width), bf16),
+            pltpu.VMEM((2, rows // 2, 16, sea_width), bf16),
+            pltpu.VMEM((2, 2, reach // 2, 16, sea_width), bf16),
             pltpu.VMEM((rows + 2 * reach, cols + 16, sea_width), f32),
-            pltpu.VMEM((2 * cols, sea_width), f32),
+            pltpu.VMEM((reach // OCEAN_DILATION * cols, sea_width), f32),
             dma((11,)),
             dma((2,)),
             dma((2, 2)),
@@ -1153,7 +1177,7 @@
         quad_weight[None, :],
         spec_real,
         spec_imag,
-        degree_gain[None, :],
+        degree_gain,
         atm_gain,
         atm_up,
         atm_down,

time: 122 us -> 101 us (0.83)
  Pallas kernels: 116 us -> 96.4 us
  local copies, waits for them, and re-layouts: 4.61 us -> 3.36 us
    pallas_call x1, Pallas kernels: 116 us -> 96.4 us  [whole_step(): pl.pallas_call(functools.partial(whole_step_body, lat_total), out_shape=(...]
    broadcast_in_dim x1 -> x0, local copies, waits for them, and re-layouts: 1.25 us -> none  [whole_step(): degree_gain[None, :]]
where the time goes in v2:
time: 101 us; the launch traced here: 100 us
  Pallas kernels  96.4 us (95%)
  local copies, waits for them, and re-layouts  3.36 us (3%)
    pallas_call x1, Pallas kernels, whole_step(): pl.pallas_call(functools.partial(whole_step_body, lat_total), out_shape=(...  96.4 us
    unnamed x4, local copies, waits for them, and re-layouts  3.36 us

profile of v2, /device:TPU:13, one launch (start us, length us, event | category | flops | bytes accessed | tf_op | source)
XLA Modules:
  0.0 100.4 jit_solution(12949929974116963668)
XLA Ops:
  0.6 96.4 %shard_map.212 = (bf16[24,64,384]{2,1,0:T(8,128)(2,1)}, bf16[12,128,256]{2,1,0:T(8,128)(2,1)}) custom-call(bf16[24,64,384]{2,1,0:T(8,128)(2,1)} %atm_hbm.1, bf16[12,128,256]{2,1,0:T(8,128)(2,1)} %sea_hbm.1, s32[12,128]{1,0:T(8,128)} %wet_ref.1, bf16[16,192,384]{2,1,0:T(8,128)(2,1)} %bitcast.5, f32[1,192]{1,0:T(1,128)} %bitcast.9, bf16[384,384]{1,0:T(8,128)(2,1)} %real_hbm.1, ...), custom_call_target="tpu_custom_call" | custom-call | tf_op jit(solution)/shard_map/pallas_call | solution.py:1100
  97.0 0.0 copy-start
  97.0 2.5 %copy.25 = bf16[24,64,384]{2,1,0:T(8,128)(2,1)} copy(bf16[24,64,384]{2,1,0:T(8,128)(2,1)} %get-tuple-element.4) | data formatting | bytes 2359296
  99.5 0.0 copy-done
  99.5 0.9 copy.26
Async XLA Ops:
  97.0 2.5 %copy-start = (bf16[12,128,256]{2,1,0:T(8,128)(2,1)S(1)}, bf16[12,128,256]{2,1,0:T(8,128)(2,1)}, u32[]{:S(2)}) copy-start(bf16[12,128,256]{2,1,0:T(8,128)(2,1)} %get-tuple-element.5) | copy-start | bytes 2359300

commit v3 on v2

--- a/solution.py
+++ b/solution.py
@@ -357,27 +357,37 @@
     lat_total,
     atm_hbm,
     sea_hbm,
-    wet_ref,
+    wet_hbm,
     legendre_hbm,
-    quad_ref,
+    quad_hbm,
     real_hbm,
     imag_hbm,
+    degree_hbm,
+    gain_hbm,
+    up_hbm,
+    down_hbm,
+    to_sea_hbm,
+    from_sea_hbm,
+    to_air_hbm,
+    from_air_hbm,
+    taps_in_hbm,
+    sea_gain_hbm,
+    sea_up_hbm,
+    sea_down_hbm,
+    waves_hbm,
+    waves_back_hbm,
+    air_out,
+    sea_out,
+    wet_ref,
+    quad_ref,
     degree_ref,
     gain_ref,
-    up_hbm,
-    down_hbm,
     to_sea_ref,
     from_sea_ref,
     to_air_ref,
     from_air_ref,
     taps_in_ref,
     sea_gain_ref,
-    sea_up_hbm,
-    sea_down_hbm,
-    waves_hbm,
-    waves_back_hbm,
-    air_out,
-    sea_out,
     air,
     sea,
     legendre,
@@ -425,13 +435,9 @@
     local_sem,
     flux_sem,
     column_sem,
-    column_own,
     owner_sem,
-    owner_own,
     back_sem,
-    back_own,
     grid_sem,
-    grid_own,
     op_sem,
     halo_sem,
 ):
@@ -475,20 +481,22 @@
     def across(left, right):
         return lax.dot_general(left, right, (((1,), (1,)), ((), ())), preferred_element_type=f32)
 
-    barrier = pltpu.get_barrier_semaphore()
-
-    @pl.loop(1, devices)
-    def _(k):
-        pl.semaphore_signal(
-            barrier, inc=1, device_id=at_device((me + k) % devices), device_id_type=MESH_ID
-        )
-
     loads = {}
     for index, (name, source, target) in enumerate(
         (
             ("legendre", legendre_hbm, legendre),
+            ("degree", degree_hbm, degree_ref),
+            ("to_air", to_air_hbm, to_air_ref),
+            ("wet", wet_hbm, wet_ref),
             ("sea", sea_hbm, sea),
+            ("to_sea", to_sea_hbm, to_sea_ref),
             ("air", atm_hbm, air),
+            ("from_sea", from_sea_hbm, from_sea_ref),
+            ("gain", gain_hbm, gain_ref),
+            ("from_air", from_air_hbm, from_air_ref),
+            ("taps", taps_in_hbm, taps_in_ref),
+            ("quad", quad_hbm, quad_ref),
+            ("sea_gain", sea_gain_hbm, sea_gain_ref),
             ("waves", waves_hbm, waves),
             ("sea_up", sea_up_hbm, sea_up),
             ("sea_down", sea_down_hbm, sea_down),
@@ -500,22 +508,20 @@
         )
     ):
         loads[name] = pltpu.make_async_copy(source, target, load_sem.at[index])
-    for name in ("legendre", "sea", "air"):
+    early = 13
+    for name in list(loads)[:early]:
         loads[name].start()
 
-    wet_square[...] = jnp.zeros_like(wet_square)
-    wet_square[0:rows, :] = wet_ref[...].astype(f32)
-    turned = jnp.transpose(wet_square[...])
-    for i in range(rows):
-        wet_full[i] = jnp.broadcast_to(turned[:, i : i + 1], (cols, 128))
-
-    for a in range(STENCIL_TAPS):
-        for b in range(STENCIL_TAPS):
-            line = taps_in_ref[a, b].astype(f32)
-            for k in range(2):
-                taps[(k * STENCIL_TAPS + a) * STENCIL_TAPS + b] = line[k : k + 1]
+    barrier = pltpu.get_barrier_semaphore()
+
+    @pl.loop(1, devices)
+    def _(k):
+        pl.semaphore_signal(
+            barrier, inc=1, device_id=at_device((me + k) % devices), device_id_type=MESH_ID
+        )
 
     loads["legendre"].wait()
+    loads["degree"].wait()
     kind = me // group
     odd = kind % 2
     place = me % group
@@ -608,7 +614,15 @@
         op_first[1].wait()
         sum_operators(odd)
 
+    loads["wet"].wait()
+    wet_square[...] = jnp.zeros_like(wet_square)
+    wet_square[0:rows, :] = wet_ref[...].astype(f32)
+    turned = jnp.transpose(wet_square[...])
+    for i in range(rows):
+        wet_full[i] = jnp.broadcast_to(turned[:, i : i + 1], (cols, 128))
+
     loads["sea"].wait()
+    loads["to_air"].wait()
 
     few = rows // 3
     for part in range(3):
@@ -627,6 +641,7 @@
         )
     moves[0].start()
     loads["air"].wait()
+    loads["to_sea"].wait()
 
     for part in range(4):
         here = slice(part * rows // 2, (part + 1) * rows // 2)
@@ -643,30 +658,31 @@
             )
         )
         kept[-1].start()
-    for name in (
-        "waves", "sea_up", "sea_down", "real", "imag", "back", "up", "down"
-    ):
+    for name in list(loads)[early:]:
         loads[name].start()
+    loads["from_sea"].wait()
+    loads["gain"].wait()
     for move in kept:
         move.wait()
     moves[0].wait()
 
 
-    def column_moves(p):
-        found = []
+    def start_columns(p):
         for k in range(1, col_count):
             other = (col + k) % col_count
-            found.append(
-                remote(
-                    normed.at[p, other],
-                    columns.at[p, col],
-                    column_sem,
-                    (p, k - 1),
-                    (lat, other // 2, other % 2),
-                )
-            )
-        own = pltpu.make_async_copy(normed.at[p, col], columns.at[p, col], column_own.at[p])
-        return found + [own]
+            remote(
+                normed.at[p, other],
+                columns.at[p, col],
+                column_sem,
+                p,
+                (lat, other // 2, other % 2),
+            ).start()
+        pltpu.make_async_copy(normed.at[p, col], columns.at[p, col], column_sem.at[1, p]).start()
+
+    def wait_columns(p):
+        sent = normed.at[p, pl.ds(0, col_count - 1)]
+        remote(sent, sent, column_sem, p, at_device(me)).wait_send()
+        pltpu.make_async_copy(columns.at[p], columns.at[p], column_sem.at[1, p]).wait()
 
     half_block = 2 * lon_dev
     for p in range(pairs):
@@ -683,9 +699,9 @@
                 value = layer_norm(value, gain_ref[0:1]).astype(bf16)
                 normed[p, j] = value.reshape(2, lon_dev, width)
 
-        for move in column_moves(p):
-            move.start()
-
+        start_columns(p)
+
+    loads["from_air"].wait()
     moves[1].wait()
 
     @pl.loop(0, rows)
@@ -792,12 +808,22 @@
 
     send_halo(0)
     op_first[1].start()
+    loads["taps"].wait()
+    loads["quad"].wait()
+    loads["sea_gain"].wait()
+
+    for a in range(STENCIL_TAPS):
+        for b in range(STENCIL_TAPS):
+            line = taps_in_ref[a, b].astype(f32)
+            for k in range(2):
+                taps[(k * STENCIL_TAPS + a) * STENCIL_TAPS + b] = line[k : k + 1]
+
     fill_operators(2 * high_half)
 
     triple = reach // step
     slab = cols // 2
 
-    def sea_half(k, upper_half):
+    def sea_half(k, upper_half, after=None):
         @pl.loop(0, step)
         def _(parity):
             base = upper_half * reach + parity
@@ -835,38 +861,30 @@
                     mask = jnp.concatenate([mask, mask], axis=1)
                     sea_out[row] = jnp.where(mask > 0.5, value, sea[row])
 
-    def exchange(source, target, sems, own_sems):
-        def away(p, k):
-            other = (me + k) % devices
-            return remote(
-                source.at[p, other], target.at[p, me], sems, (p, k), at_device(other)
-            )
-
-        def own(p):
-            return pltpu.make_async_copy(source.at[p, me], target.at[p, me], own_sems.at[p])
-
+            if after is not None:
+                after(parity)
+
+    def exchange(source, target, sems):
         def start(p):
             @pl.loop(1, devices)
             def _(k):
-                away(p, k).start()
-
-            own(p).start()
+                other = (me + k) % devices
+                remote(source.at[p, other], target.at[p, me], sems, p, at_device(other)).start()
+
+            pltpu.make_async_copy(source.at[p, me], target.at[p, me], sems.at[1, p]).start()
 
         def wait(p):
-            own(p).wait()
-
-            @pl.loop(1, devices)
-            def _(k):
-                away(p, k).wait()
+            sent = source.at[p, pl.ds(0, devices - 1)]
+            remote(sent, sent, sems, p, at_device(me)).wait_send()
+            pltpu.make_async_copy(target.at[p], target.at[p], sems.at[1, p]).wait()
 
         return start, wait
 
-    start_owner, wait_owner = exchange(spec_send, gathered, owner_sem, owner_own)
+    start_owner, wait_owner = exchange(spec_send, gathered, owner_sem)
     loads["waves"].wait()
 
     for p in range(pairs):
-        for move in column_moves(p):
-            move.wait()
+        wait_columns(p)
         found = []
         for which in range(2):
             lines = jnp.concatenate([columns[p, b, which] for b in range(col_count)], axis=0)
@@ -988,66 +1006,82 @@
                             at : at + devices, c * 128 : (c + 1) * 128
                         ]
 
-    start_back, wait_back = exchange(filtered, returned, back_sem, back_own)
-    for p in range(pairs):
+    start_back, wait_back = exchange(filtered, returned, back_sem)
+
+    def send_back(p):
         value = jnp.concatenate([flat[p, c] for c in range(lane_parts)], axis=1)
         filtered[p] = value.astype(bf16).reshape(devices, 16, width)
         start_back(p)
 
+    def send_later(parity):
+        for p in range(1, pairs):
+
+            @pl.when(parity == p - 1)
+            def _():
+                send_back(p)
+
+    send_back(0)
     take_near(1)
-    sea_half(1, 1 - comp)
-
-    def grid_moves(p):
-        found = []
+    sea_half(1, 1 - comp, send_later)
+
+    def start_grid(p, which):
+        sems = grid_sem
         for k in range(1, col_count):
             other = (col + k) % col_count
-            found.append(
-                remote(
-                    spatial.at[p, other],
-                    spectral.at[p, col],
-                    grid_sem,
-                    (p, k - 1),
-                    (lat, other // 2, other % 2),
-                )
-            )
-        own = pltpu.make_async_copy(spatial.at[p, col], spectral.at[p, col], grid_own.at[p])
-        return found + [own]
+            remote(
+                spatial.at[p, other, which],
+                spectral.at[p, col, which],
+                sems,
+                2 * p + which,
+                (lat, other // 2, other % 2),
+            ).start()
+        pltpu.make_async_copy(
+            spatial.at[p, col, which], spectral.at[p, col, which], sems.at[1, 2 * p + which]
+        ).start()
+
+    def wait_grid(p, which):
+        sent = spatial.at[p, pl.ds(0, col_count - 1), which]
+        remote(sent, sent, grid_sem, 2 * p + which, at_device(me)).wait_send()
+        here = spectral.at[p, :, which]
+        pltpu.make_async_copy(here, here, grid_sem.at[1, 2 * p + which]).wait()
 
     def to_grid(p):
         wait_back(p)
-        value = returned[p].astype(f32)
         for which in range(2):
-            lines = value[:, 8 * which : 8 * which + 8].reshape(circle, width).astype(bf16)
+            lines = returned[p, :, 8 * which : 8 * which + 8].astype(f32)
+            lines = lines.reshape(circle, width).astype(bf16)
             line = jnp.dot(waves_back[...], lines, preferred_element_type=f32).astype(bf16)
             for b in range(col_count):
                 spatial[p, b, which] = line[b * lon_dev : (b + 1) * lon_dev]
-        for move in grid_moves(p):
-            move.start()
+            start_grid(p, which)
 
     def finish(p):
-        for move in grid_moves(p):
-            move.wait()
-
-        @pl.loop(0, col_count // 2)
-        def _(jj):
-            here = pl.ds(2 * jj, 2)
-            value = forced[p, here].reshape(2 * half_block, width)
-            value = value + spectral[p, here].reshape(2 * half_block, width).astype(f32)
+
+        @pl.loop(0, 2)
+        def _(which):
+            wait_grid(p, which)
+            value = forced[p, :, which].reshape(col_count * lon_dev, width)
+            value = value + spectral[p, :, which].reshape(col_count * lon_dev, width).astype(f32)
             inner = layer_norm(value, gain_ref[1:2]).astype(bf16)
             hidden = jax.nn.gelu(
                 jnp.dot(inner, air_up[...], preferred_element_type=f32)
             ).astype(bf16)
             value = value + jnp.dot(hidden, air_down[...], preferred_element_type=f32)
-            value = value.astype(bf16).reshape(2, 2, lon_dev, width)
-            for j2 in range(2):
-                air_out[pl.ds(band * (2 * jj + j2) + 2 * p, 2)] = value[j2]
+            value = value.astype(bf16).reshape(col_count, lon_dev, width)
+            for j in range(col_count):
+                air_out[band * j + 2 * p + which] = value[j]
 
     loads["back"].wait()
     loads["up"].wait()
     loads["down"].wait()
-    to_grid(0)
     take_far(1)
-    sea_half(1, comp)
+
+    def between(parity):
+        @pl.when(parity == 0)
+        def _():
+            to_grid(0)
+
+    sea_half(1, comp, between)
     to_grid(1)
     finish(0)
     to_grid(2)
@@ -1100,15 +1134,24 @@
     return pl.pallas_call(
         functools.partial(whole_step_body, lat_total),
         out_shape=(
-            jax.ShapeDtypeStruct(atm_state.shape, bf16),
-            jax.ShapeDtypeStruct(ocean_state.shape, bf16),
+            pltpu.VMEM(atm_state.shape, bf16),
+            pltpu.VMEM(ocean_state.shape, bf16),
         ),
         in_specs=[
-            hbm, hbm, vmem, hbm, vmem, hbm, hbm, vmem, vmem, hbm, hbm,
-            vmem, vmem, vmem, vmem, vmem, vmem, hbm, hbm, hbm, hbm,
-        ],
+            hbm
+        ] * 21,
         out_specs=(vmem, vmem),
         scratch_shapes=[
+            pltpu.VMEM(wet_mask.shape, jnp.int32),
+            pltpu.VMEM((1, lat_total), f32),
+            pltpu.VMEM(degree_gain.shape, f32),
+            pltpu.VMEM(atm_gain.shape, f32),
+            pltpu.VMEM(atm_to_surface.shape[::-1], bf16),
+            pltpu.VMEM(surface_to_atm.shape, bf16),
+            pltpu.VMEM(ocean_to_surface.shape[::-1], bf16),
+            pltpu.VMEM(surface_to_ocean.shape, bf16),
+            pltpu.VMEM((STENCIL_TAPS, STENCIL_TAPS, 2, sea_width), bf16),
+            pltpu.VMEM(ocean_gain.shape, f32),
             pltpu.VMEM(atm_state.shape, bf16),
             pltpu.VMEM(ocean_state.shape, bf16),
             pltpu.VMEM((legendre.shape[0], lat_total, legendre.shape[1]), bf16),
@@ -1152,22 +1195,18 @@
             pltpu.VMEM((2, 2, reach // 2, 16, sea_width), bf16),
             pltpu.VMEM((rows + 2 * reach, cols + 16, sea_width), f32),
             pltpu.VMEM((reach // OCEAN_DILATION * cols, sea_width), f32),
-            dma((11,)),
+            dma((21,)),
             dma((2,)),
             dma((2, 2)),
-            dma((2, pairs, 3)),
-            dma((pairs,)),
-            dma((2, pairs, devices)),
-            dma((pairs,)),
-            dma((2, pairs, devices)),
-            dma((pairs,)),
-            dma((2, pairs, 3)),
-            dma((pairs,)),
+            dma((2, pairs)),
+            dma((2, pairs)),
+            dma((2, pairs)),
+            dma((2, 2 * pairs)),
             dma((2, 5)),
             dma((2, 2, 5)),
         ],
         compiler_params=pltpu.CompilerParams(
-            collective_id=0, has_side_effects=True, vmem_limit_bytes=60 * 1024 * 1024
+            collective_id=0, has_side_effects=True, vmem_limit_bytes=56 * 1024 * 1024
         ),
     )(
         atm_state,

time: 101 us -> 92.6 us (0.917)
  Pallas kernels: 96.4 us -> 89.9 us
  local copies, waits for them, and re-layouts: 3.36 us -> 1.89 us
    pallas_call x1, Pallas kernels: 96.4 us -> 89.9 us  [whole_step(): pl.pallas_call(functools.partial(whole_step_body, lat_total), out_shape=(...]
    unnamed x4 -> x2, local copies, waits for them, and re-layouts: 3.36 us -> 1.89 us
where the time goes in v3:
time: 92.6 us; the launch traced here: 92.5 us
  Pallas kernels  89.9 us (97%)
  local copies, waits for them, and re-layouts  1.89 us (2%)
    pallas_call x1, Pallas kernels, whole_step(): pl.pallas_call(functools.partial(whole_step_body, lat_total), out_shape=(...  89.9 us
    unnamed x2, local copies, waits for them, and re-layouts  1.89 us

profile of v3, /device:TPU:13, one launch (start us, length us, event | category | flops | bytes accessed | tf_op | source)
XLA Modules:
  0.0 92.5 jit_solution(4946225141320224072)
XLA Ops:
  0.6 89.9 %shard_map.212 = (bf16[24,64,384]{2,1,0:T(8,128)(2,1)S(1)}, bf16[12,128,256]{2,1,0:T(8,128)(2,1)S(1)}) custom-call(bf16[24,64,384]{2,1,0:T(8,128)(2,1)} %atm_hbm.1, bf16[12,128,256]{2,1,0:T(8,128)(2,1)} %sea_hbm.1, s32[12,128]{1,0:T(8,128)} %wet_hbm.1, bf16[16,192,384]{2,1,0:T(8,128)(2,1)} %bitcast.5, f32[1,192]{1,0:T(1,128)} %bitcast.9, ...), custom_call_target="tpu_custom_call" | custom-call | tf_op jit(solution)/shard_map/pallas_call | solution.py:1134
  90.6 1.0 %copy.25 = bf16[24,64,384]{2,1,0:T(8,128)(2,1)} copy(bf16[24,64,384]{2,1,0:T(8,128)(2,1)S(1)} %get-tuple-element.2) | data formatting | bytes 2359296
  91.6 0.9 copy.26
